TPU v7x, 32 devices: a whole 2x2x4 slice. The times are simulated.
32 devices in a mesh: loop: 8 (over y, x, core), tp: 4 (over z).
Axes of the slice: x: 2, y: 2, z: 4, core: 2. Of those that a mesh axis runs over, the one named last changes fastest.
Arguments:
- tokens: bfloat16 [2048, 4096], P('loop', 'tp'), may hold values from -6 to 6
- out_grad: bfloat16 [2048, 6144], P('loop', 'tp'), may hold values from -6 to 6
- qkv_weight: bfloat16 [3, 4096, 6144], P(None, 'loop', 'tp'), may hold values from -0.09375 to 0.09375
- dest_row: int32 [2048], P('loop'), may hold values from 0 to 383, as said below
- loop_modality: int32 [8], replicated, may hold values from 0 to 2, as said below
Outputs:
- projected: bfloat16 [2048, 6144], P('loop', 'tp')
- input_grad: bfloat16 [2048, 4096], P('loop', 'tp')
- weight_grad: bfloat16 [3, 4096, 6144], P(None, 'loop', 'tp')
Inputs may be any that keep to these rules, and one draw needn't show every extreme that they name: `dest_row`: within each aligned block of 256 tokens the values are distinct, so at most 48 tokens of one block name one loop; in every draw some loop is named by exactly 48 tokens of every block. `loop_modality`: A quarter of the loops hold 0, half hold 1, a quarter hold 2.
All inputs are finite; a program needn't handle non-finite values.
Results may differ from a plain program's by a relative error of at most 0.014.
Values may be sent and summed in bfloat16 or wider, within the bound.
No kernel may reach another device: no remote copies, remote signals or barrier semaphores. Data moves between devices by JAX's collectives and lax.ppermute only.
A program may use at most 128 MiB of HBM per device.

v0:
```python
import functools
import math

import jax
import jax.numpy as jnp
from jax import lax
from jax.experimental import pallas as pl
from jax.experimental.pallas import tpu as pltpu
from jax.sharding import PartitionSpec as P


BF16 = jnp.bfloat16
F32 = jnp.float32


def kind_kernel(kinds_of_loops, dest, out, *, capacity):
    slots = dest[...]
    found = jnp.full(slots.shape, kinds_of_loops[0], jnp.int32)
    for loop_index in range(1, kinds_of_loops.shape[0]):
        found = jnp.where(slots >= loop_index * capacity, kinds_of_loops[loop_index], found)
    out[...] = found


def modality_of(dest_row, loop_modality, capacity):
    slots = dest_row.reshape(1, -1)
    return pl.pallas_call(
        functools.partial(kind_kernel, capacity=capacity),
        out_shape=jax.ShapeDtypeStruct(slots.shape, jnp.int32),
        in_specs=[pl.BlockSpec(memory_space=pltpu.SMEM), pl.BlockSpec(memory_space=pltpu.VMEM)],
        out_specs=pl.BlockSpec(memory_space=pltpu.VMEM),
    )(loop_modality, slots)


def pick(kind, products):
    chosen = products[0]
    for index in range(1, len(products)):
        chosen = jnp.where(kind == index, products[index], chosen)
    return chosen


def whole(shape):
    return pl.BlockSpec(shape, lambda *_: (0,) * len(shape))


def split_rows(value, outs):
    start = 0
    for out in outs:
        yield out, value[start:start + out.shape[0]]
        start += out.shape[0]


def limit(mebibytes):
    return pltpu.CompilerParams(vmem_limit_bytes=mebibytes << 20)


def input_kernel(core, kind, own_weight, other_weight, *refs, blocks, tile):
    rhs = jnp.concatenate([ref[...] for ref in refs[:blocks]], axis=0)
    outs = refs[blocks:]
    half = outs[0].shape[1] // 2
    kinds, _, columns = own_weight.shape
    for weight, side in ((own_weight, core[0]), (other_weight, 1 - core[0])):
        product = lax.dot_general(
            weight[...].reshape(kinds * tile, columns), rhs, (((1,), (1,)), ((), ())),
            preferred_element_type=F32,
        )
        products = [product[index * tile:(index + 1) * tile] for index in range(kinds)]
        chosen = pick(kind[...], products).astype(BF16).T
        at = pl.multiple_of(side * half + pl.program_id(0) * tile, tile)
        for out, part in split_rows(chosen, outs):
            out[:, pl.ds(at, tile)] = part


def input_terms(core, kind, blocks, sizes, own_weight, other_weight):
    kinds, half, columns = own_weight.shape
    tile = min(half, 256)
    weight_spec = pl.BlockSpec((kinds, tile, columns), lambda step, core: (0, step, 0))
    return pl.pallas_call(
        functools.partial(input_kernel, blocks=len(blocks), tile=tile),
        grid_spec=pltpu.PrefetchScalarGridSpec(
            num_scalar_prefetch=1,
            grid=(half // tile,),
            in_specs=[whole(kind.shape), weight_spec, weight_spec] + [whole(block.shape) for block in blocks],
            out_specs=[whole((size, 2 * half)) for size in sizes],
        ),
        out_shape=[jax.ShapeDtypeStruct((size, 2 * half), BF16) for size in sizes],
        compiler_params=limit(28),
    )(core, kind, own_weight, other_weight, *blocks)


def project_kernel(core, kind, own_weight, other_weight, *refs, blocks):
    _, half, tile = own_weight.shape
    own_at = pl.multiple_of(core[0] * half, half)
    other_at = pl.multiple_of((1 - core[0]) * half, half)
    own = jnp.concatenate([ref[:, pl.ds(own_at, half)] for ref in refs[:blocks]], axis=0)
    other = jnp.concatenate([ref[:, pl.ds(other_at, half)] for ref in refs[:blocks]], axis=0)
    row_kind = jnp.broadcast_to(kind[...], (tile, own.shape[0])).T
    products = [
        jnp.dot(own, own_weight[index], preferred_element_type=F32)
        + jnp.dot(other, other_weight[index], preferred_element_type=F32)
        for index in range(own_weight.shape[0])
    ]
    chosen = pick(row_kind, products).astype(BF16)
    for out, part in split_rows(chosen, refs[blocks:]):
        out[...] = part


def project_parts(core, kind, blocks, sizes, own_weight, other_weight):
    kinds, half, columns = own_weight.shape
    tile = math.gcd(columns, 512)
    weight_spec = pl.BlockSpec((kinds, half, tile), lambda step, core: (0, 0, step))
    return pl.pallas_call(
        functools.partial(project_kernel, blocks=len(blocks)),
        grid_spec=pltpu.PrefetchScalarGridSpec(
            num_scalar_prefetch=1,
            grid=(columns // tile,),
            in_specs=[whole(kind.shape), weight_spec, weight_spec] + [whole(block.shape) for block in blocks],
            out_specs=[pl.BlockSpec((size, tile), lambda step, core: (0, step)) for size in sizes],
        ),
        out_shape=[jax.ShapeDtypeStruct((size, columns), BF16) for size in sizes],
        compiler_params=limit(28),
    )(core, kind, own_weight, other_weight, *blocks)


def choose_kernel(wanted, *refs, sources):
    outs = refs[sources:]
    for place, out in enumerate(outs):
        for index, source in enumerate(refs[:sources]):
            @pl.when(wanted[place] == index)
            def _(out=out, source=source):
                out[...] = source[...]


def choose(wanted, sources, count):
    rows, columns = sources[0].shape
    step_rows = rows // 4
    spec = pl.BlockSpec((step_rows, columns), lambda step, wanted: (step, 0))
    return pl.pallas_call(
        functools.partial(choose_kernel, sources=len(sources)),
        grid_spec=pltpu.PrefetchScalarGridSpec(
            num_scalar_prefetch=1,
            grid=(4,),
            in_specs=[spec] * len(sources),
            out_specs=[spec] * count,
        ),
        out_shape=[jax.ShapeDtypeStruct((rows, columns), sources[0].dtype)] * count,
        compiler_params=limit(16),
    )(wanted, *sources)


def weight_kernel(core, kind, *refs, blocks, grads, scale):
    rows = refs[:blocks]
    cotangents = refs[blocks:blocks + grads]
    out, turned = refs[blocks + grads:]
    kinds, half, _ = out.shape

    @pl.when(pl.program_id(0) == 0)
    def _():
        start = 0
        for ref in rows:
            count = ref.shape[0]
            part = ref[:, pl.ds(pl.multiple_of(core[0] * half, half), half)].T
            own_kind = kind[:, start:start + count]
            for which in range(kinds):
                turned[which, :, start:start + count] = jnp.where(own_kind == which, part, 0)
            start += count

    columns = jnp.concatenate([ref[...] for ref in cotangents], axis=0)
    for which in range(kinds):
        total = jnp.dot(turned[which], columns, preferred_element_type=F32)
        out[which] = (total * scale).astype(BF16)


def weight_gradient(core, kind, blocks, grads, kinds, scale):
    half = blocks[0].shape[1] // 2
    columns = grads[0].shape[1]
    tile = min(columns, 256)
    rows = kind.shape[1]
    return pl.pallas_call(
        functools.partial(weight_kernel, blocks=len(blocks), grads=len(grads), scale=scale),
        grid_spec=pltpu.PrefetchScalarGridSpec(
            num_scalar_prefetch=1,
            grid=(columns // tile,),
            in_specs=[whole(kind.shape)]
            + [whole(block.shape) for block in blocks]
            + [pl.BlockSpec((block.shape[0], tile), lambda step, core: (0, step)) for block in grads],
            out_specs=pl.BlockSpec((kinds, half, tile), lambda step, core: (0, 0, step)),
            scratch_shapes=[pltpu.VMEM((kinds, half, rows), BF16)],
        ),
        out_shape=jax.ShapeDtypeStruct((kinds, half, columns), BF16),
        compiler_params=limit(36),
    )(core, kind, *blocks, *grads)


def low_high(offset):
    return offset & -offset, 1 << (offset.bit_length() - 1)


def body(tokens, out_grad, qkv_weight, dest_row, loop_modality):
    loop_count = lax.axis_size("loop")
    tp_count = lax.axis_size("tp")
    row_count, feature_part = tokens.shape
    kinds, half, _ = qkv_weight.shape
    chip_count = loop_count // 2
    assert chip_count == tp_count and 2 * half == feature_part
    capacity = 3 * row_count // (2 * loop_count)
    grad_scale = 1.0 / math.sqrt(row_count * loop_count)
    loop_index = lax.axis_index("loop")
    chip, level = loop_index >> 1, lax.axis_index("tp")
    core = (loop_index & 1).reshape(1)
    bits = [1 << place for place in range(chip_count.bit_length() - 1)]
    offsets = sorted(range(1, chip_count), key=lambda offset: (bin(offset).count("1"), offset))
    several = [offset for offset in offsets if offset & (offset - 1)]
    cut = row_count // 2

    def across(value, offset):
        pairs = [(i, i ^ (2 * offset)) for i in range(loop_count)]
        return lax.ppermute(value, "loop", pairs)

    def sibling(value):
        return lax.ppermute(value, "loop", [(i, i ^ 1) for i in range(loop_count)])

    def line_pairs(parity, stage):
        pairs = []
        for low in range(parity, tp_count - 1, 2):
            if low - stage + 1 >= 0:
                pairs.append((low, low + 1))
            if low + stage <= tp_count - 1:
                pairs.append((low + 1, low))
        return pairs

    def along(value, pairs):
        return lax.ppermute(value, "tp", pairs)

    stages = range(1, tp_count)
    facing = [jnp.where(level % 2 == parity, 1, -1) for parity in (0, 1)]

    other_weight = sibling(qkv_weight)
    came = {(0, 0): tokens, (1, 0): tokens}
    for stage in stages:
        for parity in (0, 1):
            pairs = line_pairs(parity, stage)
            if pairs:
                came[parity, stage] = along(came[1 - parity, stage - 1], pairs)

    own_grad = [out_grad[:cut], out_grad[cut:]]
    grads = {0: own_grad}
    for bit in bits:
        grads[bit] = [None, None]
    for bit in bits:
        first = 0 if bit == bits[-1] else 1
        for part in (first, 1 - first):
            grads[bit][part] = across(own_grad[part], bit)
    for offset in several:
        low, high = low_high(offset)
        grads[offset] = [across(grads[offset ^ low][0], low), across(grads[offset ^ high][1], high)]

    own_kind = modality_of(dest_row, loop_modality, capacity)
    kind = own_kind
    for bit in bits:
        kind = jnp.concatenate([kind, across(kind, bit)], axis=0)
    other_kind = sibling(kind)
    kind_of = [own_kind] + [kind[offset:offset + 1] for offset in range(1, chip_count)]

    def group_kind(group):
        return jnp.concatenate([kind_of[offset] for offset in group], axis=1)

    arrived = {}
    for group in ([0], bits, several):
        blocks = [out_grad] if group == [0] else [part for offset in group for part in grads[offset]]
        made = input_terms(core, group_kind(group), blocks, [row_count] * len(group), qkv_weight, other_weight)
        for offset, term in zip(group, made):
            arrived[offset] = across(term, offset) if offset else term
    all_terms = [arrived[offset] for offset in range(chip_count)]

    def level_term(where):
        offset = chip ^ jnp.clip(where, 0, tp_count - 1)
        term = all_terms[0]
        for index in range(1, chip_count):
            term = jnp.where(offset == index, all_terms[index], term)
        return term.astype(F32)

    back = {}
    for stage in reversed(stages):
        for parity in (0, 1):
            pairs = line_pairs(parity, stage)
            if pairs:
                value = level_term(level + stage * facing[parity])
                if (1 - parity, stage + 1) in back:
                    value = value + back[1 - parity, stage + 1].astype(F32)
                back[parity, stage] = along(value.astype(BF16), [(b, a) for a, b in pairs])
    input_grad = level_term(level)
    for parity in (0, 1):
        if (parity, 1) in back:
            input_grad = input_grad + back[parity, 1].astype(F32)
    input_grad = input_grad.astype(BF16)

    places = [place for place in came if place != (1, 0)]
    sources = [came[place] for place in places]
    wanted = []
    for offset in range(chip_count):
        where = chip ^ offset
        index = jnp.int32(0)
        for number, (parity, stage) in enumerate(places):
            if stage:
                index = jnp.where(where == level + stage * facing[parity], number, index)
        wanted.append(index)
    sends = choose(jnp.stack(wanted), sources, chip_count)
    rows = {offset: across(sends[offset], offset) if offset else sends[offset] for offset in range(chip_count)}

    parts = {}
    for group in (several, bits + [0]):
        made = project_parts(
            core, group_kind(group), [rows[offset] for offset in group],
            [cut] * (2 * len(group)), qkv_weight, other_weight,
        )
        for place, offset in enumerate(group):
            parts[offset] = [part.astype(F32) for part in made[2 * place:2 * place + 2]]
    for offset in reversed(several):
        low, high = low_high(offset)
        for part, (near, link) in enumerate(((offset ^ low, low), (offset ^ high, high))):
            piece = across(parts[offset][part].astype(BF16), link)
            parts[near][part] = parts[near][part] + piece.astype(F32)
    for bit in bits:
        for part in (0, 1):
            piece = across(parts[bit][part].astype(BF16), bit)
            parts[0][part] = parts[0][part] + piece.astype(F32)
    projected = jnp.concatenate([part.astype(BF16) for part in parts[0]], axis=0)

    near = [rows[offset] for offset in range(chip_count)]
    far = [sibling(block) for block in near]
    near_grads = [out_grad] + [part for offset in range(1, chip_count) for part in grads[offset]]
    far_grads = [sibling(block) for block in near_grads]
    all_kind = jnp.concatenate([kind.reshape(1, -1), other_kind.reshape(1, -1)], axis=1)
    weight_grad = weight_gradient(core, all_kind, near + far, near_grads + far_grads, kinds, grad_scale)
    return projected, input_grad, weight_grad


def solution(mesh):
    placed = (P("loop", "tp"), P("loop", "tp"), P(None, "loop", "tp"), P("loop"), P())
    return jax.shard_map(
        body,
        mesh=mesh,
        in_specs=placed,
        out_specs=(P("loop", "tp"), P("loop", "tp"), P(None, "loop", "tp")),
        check_vma=False,
    )
```

profile of v0, /device:TPU:0, one launch (start us, length us, event | category | flops | bytes accessed | tf_op | source)
XLA Modules:
  0.0 209.3 jit_solution(2683077773068715940)
XLA Ops:
  1.2 2.6 %collective-permute-start.3 = (bf16[256,1024]{1,0:T(8,128)(2,1)}, bf16[256,1024]{1,0:T(8,128)(2,1)S(1)}, u32[]{:S(2)}, u32[]{:S(2)}) collective-permute-start(bf16[256,1024]{1,0:T(8,128)(2,1)} %refs_0_.2), channel_id=1, source_target_pairs={{0,1},{1,0},{2,3},{3,2},{4,5},{5,4},{6,7},{7,6},{8,9},{9,8},{10,11... | collective-permute-start | bytes 1572872 | tf_op jit(solution)/shard_map/ppermute | solution.py:232
  5.0 1.6 collective-permute-start.17
  9.9 1.8 collective-permute-done
  12.8 3.5 %collective-permute-done.1 = s32[2,256]{1,0:T(2,128)S(1)} collective-permute-done((s32[2,256]{1,0:T(2,128)S(1)}, s32[2,256]{1,0:T(2,128)S(1)}, u32[]{:S(2)}, u32[]{:S(2)}) %collective-permute-start.1) | collective-permute-done | bytes 2080 | tf_op jit(solution)/shard_map/ppermute | solution.py:217
  21.0 1.6 collective-permute-start.23
  22.6 6.7 %collective-permute-done.22.refs_0_.refs_9_ = bf16[128,1536]{1,0:T(8,128)(2,1)S(1)} collective-permute-done((bf16[128,1536]{1,0:T(8,128)(2,1)S(1)}, bf16[128,1536]{1,0:T(8,128)(2,1)S(1)}, u32[]{:S(2)}, u32[]{:S(2)}) %collective-permute-start.22) | collective-permute-done | bytes 393248 | tf_op jit(solution)/shard_map/ppermute | solution.py:217
  35.0 4.9 %collective-permute-done.18.refs_0_.refs_13_ = bf16[128,1536]{1,0:T(8,128)(2,1)} collective-permute-done((bf16[128,1536]{1,0:T(8,128)(2,1)S(1)}, bf16[128,1536]{1,0:T(8,128)(2,1)}, u32[]{:S(2)}, u32[]{:S(2)}) %collective-permute-start.18) | collective-permute-done | bytes 393248 | tf_op jit(solution)/shard_map/ppermute | solution.py:217
  39.8 1.5 collective-permute-start.20
  41.4 8.2 %collective-permute-done.20.refs_1_.refs_14_ = bf16[128,1536]{1,0:T(8,128)(2,1)} collective-permute-done((bf16[128,1536]{1,0:T(8,128)(2,1)S(1)}, bf16[128,1536]{1,0:T(8,128)(2,1)}, u32[]{:S(2)}, u32[]{:S(2)}) %collective-permute-start.20) | collective-permute-done | bytes 393248 | tf_op jit(solution)/shard_map/ppermute | solution.py:217
  50.8 10.0 %collective-permute-done.7.refs_5_ = bf16[256,1024]{1,0:T(8,128)(2,1)S(1)} collective-permute-done((bf16[256,1024]{1,0:T(8,128)(2,1)S(1)}, bf16[256,1024]{1,0:T(8,128)(2,1)S(1)}, u32[]{:S(2)}, u32[]{:S(2)}) %collective-permute-start.7) | collective-permute-done | bytes 524320 | tf_op jit(solution)/shard_map/ppermute | solution.py:232
  66.9 2.6 %shard_map.77 = (bf16[256,1024]{1,0:T(8,128)(2,1)S(1)}, bf16[256,1024]{1,0:T(8,128)(2,1)}, bf16[256,1024]{1,0:T(8,128)(2,1)}, bf16[256,1024]{1,0:T(8,128)(2,1)S(1)}) custom-call(s32[4]{0:T(128)S(1)} %pad_add_fusion.5.wanted, bf16[256,1024]{1,0:T(8,128)(2,1)S(1)} %copy-done.11, bf16[256,1024]{1,0:T(8,128)(2,1)S(1)} %collective-permute-done.3.refs_1_, ...), custom_call_target="tpu_custom_call" | custom-call | tf_op jit(solution)/shard_map/pallas_call | solution.py:137
  71.9 2.4 %collective-permute-start.11 = (bf16[256,1024]{1,0:T(8,128)(2,1)}, bf16[256,1024]{1,0:T(8,128)(2,1)S(1)}, u32[]{:S(2)}, u32[]{:S(2)}) collective-permute-start(bf16[256,1024]{1,0:T(8,128)(2,1)} %copy-done.21), channel_id=1, source_target_pairs={{0,24},{4,28},{8,16},{12,20},{16,8},{20,12},{24,0},{28,4},{1,25},{... | collective-permute-start | bytes 1572872 | tf_op jit(solution)/shard_map/ppermute | solution.py:217
  74.3 2.3 %copy-done = bf16[3,512,1536]{2,1,0:T(8,128)(2,1)S(1)} copy-done((bf16[3,512,1536]{2,1,0:T(8,128)(2,1)S(1)}, bf16[3,512,1536]{2,1,0:T(8,128)(2,1)}, u32[]{:S(2)}) %copy-start) | copy-done | bytes 4718616
  76.7 5.8 %shard_map.80 = bf16[256,1024]{1,0:T(8,128)(2,1)} custom-call(s32[1]{0:T(128)} %bitcast.core, s32[1,256]{1,0:T(1,128)S(1)} %get-tuple-element.39.kind, bf16[3,512,1536]{2,1,0:T(8,128)(2,1)S(1)} %copy-done, bf16[3,512,1536]{2,1,0:T(8,128)(2,1)} %collective-permute-done.2.other_weight, bf16[128,1536]{1,0:T(8,128)(2,1)} %collective-permute-done.18.refs_0_.refs_13_, ...), custom_call_target="tpu_custom_call" | custom-call | tf_op jit(solution)/shard_map/pallas_call | solution.py:77
  82.5 8.4 %shard_map.81 = (bf16[256,1024]{1,0:T(8,128)(2,1)}, bf16[256,1024]{1,0:T(8,128)(2,1)}) custom-call(s32[1]{0:T(128)} %bitcast.core, s32[1,512]{1,0:T(1,128)S(1)} %pad_add_fusion.4.kind, bf16[3,512,1536]{2,1,0:T(8,128)(2,1)S(1)} %copy-done, bf16[3,512,1536]{2,1,0:T(8,128)(2,1)} %collective-permute-done.2.other_weight, bf16[128,1536]{1,0:T(8,128)(2,1)S(1)} %copy-done.7, ...), custom_call_target="tpu_custom_call" | custom-call | tf_op jit(solution)/shard_map/pallas_call | solution.py:77
  95.0 2.9 %collective-permute-done.11.refs_0_.refs_3_ = bf16[256,1024]{1,0:T(8,128)(2,1)S(1)} collective-permute-done((bf16[256,1024]{1,0:T(8,128)(2,1)}, bf16[256,1024]{1,0:T(8,128)(2,1)S(1)}, u32[]{:S(2)}, u32[]{:S(2)}) %collective-permute-start.11) | collective-permute-done | bytes 524320 | tf_op jit(solution)/shard_map/ppermute | solution.py:217
  97.9 2.3 %copy-done.1 = bf16[3,512,1536]{2,1,0:T(8,128)(2,1)S(1)} copy-done((bf16[3,512,1536]{2,1,0:T(8,128)(2,1)S(1)}, bf16[3,512,1536]{2,1,0:T(8,128)(2,1)}, u32[]{:S(2)}) %copy-start.1) | copy-done | bytes 4718616
  100.3 4.8 %shard_map.82 = bf16[256,1024]{1,0:T(8,128)(2,1)S(1)} custom-call(s32[1]{0:T(128)} %bitcast.core, s32[1,256]{1,0:T(1,128)S(1)} %copy-done.20, bf16[3,512,1536]{2,1,0:T(8,128)(2,1)S(1)} %copy-done.1, bf16[3,512,1536]{2,1,0:T(8,128)(2,1)} %collective-permute-done.2.other_weight, bf16[256,1536]{1,0:T(8,128)(2,1)S(1)} %copy-done.3), custom_call_target="tpu_custom_call" | custom-call | tf_op jit(solution)/shard_map/pallas_call | solution.py:77
  105.1 2.3 %copy-done.2 = bf16[3,512,1536]{2,1,0:T(8,128)(2,1)S(1)} copy-done((bf16[3,512,1536]{2,1,0:T(8,128)(2,1)S(1)}, bf16[3,512,1536]{2,1,0:T(8,128)(2,1)}, u32[]{:S(2)}) %copy-start.2) | copy-done | bytes 4718616
  107.5 5.1 %shard_map.79 = (bf16[128,1536]{1,0:T(8,128)(2,1)S(1)}, bf16[128,1536]{1,0:T(8,128)(2,1)S(1)}) custom-call(s32[1]{0:T(128)} %bitcast.core, s32[1,256]{1,0:T(1,128)S(1)} %get-tuple-element.39.kind, bf16[3,512,1536]{2,1,0:T(8,128)(2,1)S(1)} %copy-done.2, bf16[3,512,1536]{2,1,0:T(8,128)(2,1)} %collective-permute-done.2.other_weight, ...), custom_call_target="tpu_custom_call" | custom-call | tf_op jit(solution)/shard_map/pallas_call | solution.py:111
  112.6 7.3 %collective-permute-done.9.refs_1_.refs_2_ = bf16[256,1024]{1,0:T(8,128)(2,1)S(1)} collective-permute-done((bf16[256,1024]{1,0:T(8,128)(2,1)}, bf16[256,1024]{1,0:T(8,128)(2,1)S(1)}, u32[]{:S(2)}, u32[]{:S(2)}) %collective-permute-start.9) | collective-permute-done | bytes 524320 | tf_op jit(solution)/shard_map/ppermute | solution.py:217
  120.4 10.7 %collective-permute-done.24 = bf16[256,1024]{1,0:T(8,128)(2,1)} collective-permute-done((bf16[256,1024]{1,0:T(8,128)(2,1)}, bf16[256,1024]{1,0:T(8,128)(2,1)}, u32[]{:S(2)}, u32[]{:S(2)}) %collective-permute-start.24) | collective-permute-done | bytes 524320 | tf_op jit(solution)/shard_map/ppermute | solution.py:217
  131.7 1.5 select_select_fusion.1
  133.2 4.4 %collective-permute-start.26 = (bf16[256,1024]{1,0:T(8,128)(2,1)S(1)}, bf16[256,1024]{1,0:T(8,128)(2,1)S(1)}, u32[]{:S(2)}, u32[]{:S(2)}) collective-permute-start(bf16[256,1024]{1,0:T(8,128)(2,1)S(1)} %get-tuple-element.33), channel_id=1, source_target_pairs={{0,1},{3,2},{4,5},{7,6},{8,9},{11,10},{12,13},{15,14},{16,17},{19,... | collective-permute-start | bytes 1572872 | tf_op jit(solution)/shard_map/ppermute | solution.py:232
  137.7 14.9 %shard_map.83 = bf16[3,512,1536]{2,1,0:T(8,128)(2,1)} custom-call(s32[1]{0:T(128)} %bitcast.core, s32[1,2048]{1,0:T(1,128)S(1)} %pad_add_fusion.kind, bf16[256,1024]{1,0:T(8,128)(2,1)S(1)} %get-tuple-element.19.refs_2_.refs_0_, bf16[256,1024]{1,0:T(8,128)(2,1)S(1)} %collective-permute-done.8.refs_0_.refs_1_, ...), custom_call_target="tpu_custom_call" | custom-call | tf_op jit(solution)/shard_map/pallas_call | solution.py:178
  152.6 9.6 %shard_map.78 = (bf16[128,1536]{1,0:T(8,128)(2,1)S(1)}, bf16[128,1536]{1,0:T(8,128)(2,1)S(1)}, bf16[128,1536]{1,0:T(8,128)(2,1)S(1)}, bf16[128,1536]{1,0:T(8,128...) custom-call(s32[1]{0:T(128)} %bitcast.core, s32[1,768]{1,0:T(1,128)S(1)} %pad_add_fusion.2.kind, ...), custom_call_target="tpu_custom_call" | custom-call | tf_op jit(solution)/shard_map/pallas_call | solution.py:111
  162.2 1.6 collective-permute-start.16
  168.4 7.5 %collective-permute-done.12 = bf16[128,1536]{1,0:T(8,128)(2,1)S(1)} collective-permute-done((bf16[128,1536]{1,0:T(8,128)(2,1)S(1)}, bf16[128,1536]{1,0:T(8,128)(2,1)S(1)}, u32[]{:S(2)}, u32[]{:S(2)}) %collective-permute-start.12) | collective-permute-done | bytes 393248 | tf_op jit(solution)/shard_map/ppermute | solution.py:217
  177.2 14.2 %collective-permute-done.15 = bf16[128,1536]{1,0:T(8,128)(2,1)S(1)} collective-permute-done((bf16[128,1536]{1,0:T(8,128)(2,1)S(1)}, bf16[128,1536]{1,0:T(8,128)(2,1)S(1)}, u32[]{:S(2)}, u32[]{:S(2)}) %collective-permute-start.15) | collective-permute-done | bytes 393248 | tf_op jit(solution)/shard_map/ppermute | solution.py:217
  191.6 2.1 add_convert_fusion.2
  194.3 2.7 %collective-permute-start.28 = (bf16[256,1024]{1,0:T(8,128)(2,1)S(1)}, bf16[256,1024]{1,0:T(8,128)(2,1)S(1)}, u32[]{:S(2)}, u32[]{:S(2)}) collective-permute-start(bf16[256,1024]{1,0:T(8,128)(2,1)S(1)} %get-tuple-element.31), channel_id=1, source_target_pairs={{1,0},{0,1},{3,2},{2,3},{5,4},{4,5},{7,6},{6,7},{9,8},{8,9},{11,10... | collective-permute-start | bytes 1572872 | tf_op jit(solution)/shard_map/ppermute | solution.py:232
  198.1 9.8 %collective-permute-done.28 = bf16[256,1024]{1,0:T(8,128)(2,1)S(1)} collective-permute-done((bf16[256,1024]{1,0:T(8,128)(2,1)S(1)}, bf16[256,1024]{1,0:T(8,128)(2,1)S(1)}, u32[]{:S(2)}, u32[]{:S(2)}) %collective-permute-start.28) | collective-permute-done | bytes 524320 | tf_op jit(solution)/shard_map/ppermute | solution.py:232
  (130 shorter events, 40.7 us)
Async XLA Ops:
  0.6 71.2 %collective-permute-start.2 = (bf16[3,512,1536]{2,1,0:T(8,128)(2,1)}, bf16[3,512,1536]{2,1,0:T(8,128)(2,1)}, u32[]{:S(2)}, u32[]{:S(2)}) collective-permute-start(bf16[3,512,1536]{2,1,0:T(8,128)(2,1)} %own_weight.9), channel_id=1, source_target_pairs={{0,4},{4,0},{8,12},{12,8},{16,20},{20,16},{24,28},{28,24},{1,5},{5... | collective-permute-start | bytes 14155784 | tf_op jit(solution)/shard_map/ppermute | solution.py:220
  1.2 19.1 %collective-permute-start.3 = (bf16[256,1024]{1,0:T(8,128)(2,1)}, bf16[256,1024]{1,0:T(8,128)(2,1)S(1)}, u32[]{:S(2)}, u32[]{:S(2)}) collective-permute-start(bf16[256,1024]{1,0:T(8,128)(2,1)} %refs_0_.2), channel_id=1, source_target_pairs={{0,1},{1,0},{2,3},{3,2},{4,5},{5,4},{6,7},{7,6},{8,9},{9,8},{10,11... | collective-permute-start | bytes 1572872 | tf_op jit(solution)/shard_map/ppermute | solution.py:232
  5.0 14.6 %collective-permute-start.17 = (bf16[128,1536]{1,0:T(8,128)(2,1)S(1)}, bf16[128,1536]{1,0:T(8,128)(2,1)S(1)}, u32[]{:S(2)}, u32[]{:S(2)}) collective-permute-start(bf16[128,1536]{1,0:T(8,128)(2,1)S(1)} %get-tuple-element.36), channel_id=1, source_target_pairs={{0,16},{4,20},{8,24},{12,28},{16,0},{20,4},{24,8},{28,12},{1,17},{... | collective-permute-start | bytes 1179656 | tf_op jit(solution)/shard_map/ppermute | solution.py:217
  20.3 12.6 %collective-permute-start.6 = (bf16[256,1024]{1,0:T(8,128)(2,1)S(1)}, bf16[256,1024]{1,0:T(8,128)(2,1)S(1)}, u32[]{:S(2)}, u32[]{:S(2)}) collective-permute-start(bf16[256,1024]{1,0:T(8,128)(2,1)S(1)} %collective-permute-done.3.refs_1_), channel_id=1, source_target_pairs={{1,2},{2,1},{5,6},{6,5},{9,10},{10,9},{13,14},{14,13},{17,18},{18,... | collective-permute-start | bytes 1572872 | tf_op jit(solution)/shard_map/ppermute | solution.py:232
  21.0 13.9 %collective-permute-start.23 = (bf16[128,1536]{1,0:T(8,128)(2,1)S(1)}, bf16[128,1536]{1,0:T(8,128)(2,1)}, u32[]{:S(2)}, u32[]{:S(2)}) collective-permute-start(bf16[128,1536]{1,0:T(8,128)(2,1)S(1)} %get-tuple-element.35), channel_id=1, source_target_pairs={{0,16},{4,20},{8,24},{12,28},{16,0},{20,4},{24,8},{28,12},{1,17},{... | collective-permute-start | bytes 1179656 | tf_op jit(solution)/shard_map/ppermute | solution.py:217
  30.8 18.9 %collective-permute-start.5 = (bf16[256,1024]{1,0:T(8,128)(2,1)S(1)}, bf16[256,1024]{1,0:T(8,128)(2,1)S(1)}, u32[]{:S(2)}, u32[]{:S(2)}) collective-permute-start(bf16[256,1024]{1,0:T(8,128)(2,1)S(1)} %collective-permute-done.4.refs_2_), channel_id=1, source_target_pairs={{1,0},{2,3},{5,4},{6,7},{9,8},{10,11},{13,12},{14,15},{17,16},{18,... | collective-permute-start | bytes 1572872 | tf_op jit(solution)/shard_map/ppermute | solution.py:232
  32.9 28.0 %collective-permute-start.7 = (bf16[256,1024]{1,0:T(8,128)(2,1)S(1)}, bf16[256,1024]{1,0:T(8,128)(2,1)S(1)}, u32[]{:S(2)}, u32[]{:S(2)}) collective-permute-start(bf16[256,1024]{1,0:T(8,128)(2,1)S(1)} %collective-permute-done.6.refs_4_), channel_id=1, source_target_pairs={{1,0},{2,3},{5,4},{6,7},{9,8},{10,11},{13,12},{14,15},{17,16},{18,... | collective-permute-start | bytes 1572872 | tf_op jit(solution)/shard_map/ppermute | solution.py:232
  35.0 34.6 %collective-permute-start.36 = (bf16[256,1536]{1,0:T(8,128)(2,1)}, bf16[256,1536]{1,0:T(8,128)(2,1)S(1)}, u32[]{:S(2)}, u32[]{:S(2)}) collective-permute-start(bf16[256,1536]{1,0:T(8,128)(2,1)} %refs_8_.1), channel_id=1, source_target_pairs={{0,4},{4,0},{8,12},{12,8},{16,20},{20,16},{24,28},{28,24},{1,5},{5... | collective-permute-start | bytes 2359304 | tf_op jit(solution)/shard_map/ppermute | solution.py:220
  49.5 21.6 %collective-permute-start.37 = (bf16[128,1536]{1,0:T(8,128)(2,1)S(1)}, bf16[128,1536]{1,0:T(8,128)(2,1)}, u32[]{:S(2)}, u32[]{:S(2)}) collective-permute-start(bf16[128,1536]{1,0:T(8,128)(2,1)S(1)} %collective-permute-done.22.refs_0_.refs_9_), channel_id=1, source_target_pairs={{0,4},{4,0},{8,12},{12,8},{16,20},{20,16},{24,28},{28,24},{1,5},{5... | collective-permute-start | bytes 1179656 | tf_op jit(solution)/shard_map/ppermute | solution.py:220
  50.5 20.9 %collective-permute-start.38 = (bf16[128,1536]{1,0:T(8,128)(2,1)S(1)}, bf16[128,1536]{1,0:T(8,128)(2,1)}, u32[]{:S(2)}, u32[]{:S(2)}) collective-permute-start(bf16[128,1536]{1,0:T(8,128)(2,1)S(1)} %collective-permute-done.19.refs_1_.refs_10_), channel_id=1, source_target_pairs={{0,4},{4,0},{8,12},{12,8},{16,20},{20,16},{24,28},{28,24},{1,5},{5... | collective-permute-start | bytes 1179656 | tf_op jit(solution)/shard_map/ppermute | solution.py:220
  70.6 22.9 %collective-permute-start.8 = (bf16[256,1024]{1,0:T(8,128)(2,1)}, bf16[256,1024]{1,0:T(8,128)(2,1)S(1)}, u32[]{:S(2)}, u32[]{:S(2)}) collective-permute-start(bf16[256,1024]{1,0:T(8,128)(2,1)} %get-tuple-element.17), channel_id=1, source_target_pairs={{0,8},{4,12},{8,0},{12,4},{16,24},{20,28},{24,16},{28,20},{1,9},{5... | collective-permute-start | bytes 1572872 | tf_op jit(solution)/shard_map/ppermute | solution.py:217
  71.1 19.8 %collective-permute-start.40 = (bf16[128,1536]{1,0:T(8,128)(2,1)}, bf16[128,1536]{1,0:T(8,128)(2,1)}, u32[]{:S(2)}, u32[]{:S(2)}) collective-permute-start(bf16[128,1536]{1,0:T(8,128)(2,1)} %collective-permute-done.23.refs_3_.refs_12_), channel_id=1, source_target_pairs={{0,4},{4,0},{8,12},{12,8},{16,20},{20,16},{24,28},{28,24},{1,5},{5... | collective-permute-start | bytes 1179656 | tf_op jit(solution)/shard_map/ppermute | solution.py:220
  71.4 20.1 %collective-permute-start.41 = (bf16[128,1536]{1,0:T(8,128)(2,1)}, bf16[128,1536]{1,0:T(8,128)(2,1)}, u32[]{:S(2)}, u32[]{:S(2)}) collective-permute-start(bf16[128,1536]{1,0:T(8,128)(2,1)} %collective-permute-done.18.refs_0_.refs_13_), channel_id=1, source_target_pairs={{0,4},{4,0},{8,12},{12,8},{16,20},{20,16},{24,28},{28,24},{1,5},{5... | collective-permute-start | bytes 1179656 | tf_op jit(solution)/shard_map/ppermute | solution.py:220
  71.6 21.3 %collective-permute-start.42 = (bf16[128,1536]{1,0:T(8,128)(2,1)}, bf16[128,1536]{1,0:T(8,128)(2,1)}, u32[]{:S(2)}, u32[]{:S(2)}) collective-permute-start(bf16[128,1536]{1,0:T(8,128)(2,1)} %collective-permute-done.20.refs_1_.refs_14_), channel_id=1, source_target_pairs={{0,4},{4,0},{8,12},{12,8},{16,20},{20,16},{24,28},{28,24},{1,5},{5... | collective-permute-start | bytes 1179656 | tf_op jit(solution)/shard_map/ppermute | solution.py:220
  71.9 26.0 %collective-permute-start.11 = (bf16[256,1024]{1,0:T(8,128)(2,1)}, bf16[256,1024]{1,0:T(8,128)(2,1)S(1)}, u32[]{:S(2)}, u32[]{:S(2)}) collective-permute-start(bf16[256,1024]{1,0:T(8,128)(2,1)} %copy-done.21), channel_id=1, source_target_pairs={{0,24},{4,28},{8,16},{12,20},{16,8},{20,12},{24,0},{28,4},{1,25},{... | collective-permute-start | bytes 1572872 | tf_op jit(solution)/shard_map/ppermute | solution.py:217
  90.9 28.9 %collective-permute-start.9 = (bf16[256,1024]{1,0:T(8,128)(2,1)}, bf16[256,1024]{1,0:T(8,128)(2,1)S(1)}, u32[]{:S(2)}, u32[]{:S(2)}) collective-permute-start(bf16[256,1024]{1,0:T(8,128)(2,1)} %get-tuple-element.18), channel_id=1, source_target_pairs={{0,16},{4,20},{8,24},{12,28},{16,0},{20,4},{24,8},{28,12},{1,17},{... | collective-permute-start | bytes 1572872 | tf_op jit(solution)/shard_map/ppermute | solution.py:217
  91.5 28.4 %collective-permute-start.21 = (bf16[256,1024]{1,0:T(8,128)(2,1)}, bf16[256,1024]{1,0:T(8,128)(2,1)}, u32[]{:S(2)}, u32[]{:S(2)}) collective-permute-start(bf16[256,1024]{1,0:T(8,128)(2,1)} %shard_map.80), channel_id=1, source_target_pairs={{0,24},{4,28},{8,16},{12,20},{16,8},{20,12},{24,0},{28,4},{1,25},{... | collective-permute-start | bytes 1572872 | tf_op jit(solution)/shard_map/ppermute | solution.py:217
  92.9 38.2 %collective-permute-start.24 = (bf16[256,1024]{1,0:T(8,128)(2,1)}, bf16[256,1024]{1,0:T(8,128)(2,1)}, u32[]{:S(2)}, u32[]{:S(2)}) collective-permute-start(bf16[256,1024]{1,0:T(8,128)(2,1)} %get-tuple-element.29), channel_id=1, source_target_pairs={{0,16},{4,20},{8,24},{12,28},{16,0},{20,4},{24,8},{28,12},{1,17},{... | collective-permute-start | bytes 1572872 | tf_op jit(solution)/shard_map/ppermute | solution.py:217
  93.5 37.7 %collective-permute-start.25 = (bf16[256,1024]{1,0:T(8,128)(2,1)}, bf16[256,1024]{1,0:T(8,128)(2,1)}, u32[]{:S(2)}, u32[]{:S(2)}) collective-permute-start(bf16[256,1024]{1,0:T(8,128)(2,1)} %get-tuple-element.30), channel_id=1, source_target_pairs={{0,8},{4,12},{8,0},{12,4},{16,24},{20,28},{24,16},{28,20},{1,9},{5... | collective-permute-start | bytes 1572872 | tf_op jit(solution)/shard_map/ppermute | solution.py:217
  97.9 35.3 %collective-permute-start.32 = (bf16[256,1024]{1,0:T(8,128)(2,1)S(1)}, bf16[256,1024]{1,0:T(8,128)(2,1)}, u32[]{:S(2)}, u32[]{:S(2)}) collective-permute-start(bf16[256,1024]{1,0:T(8,128)(2,1)S(1)} %get-tuple-element.19.refs_2_.refs_0_), channel_id=1, source_target_pairs={{0,4},{4,0},{8,12},{12,8},{16,20},{20,16},{24,28},{28,24},{1,5},{5... | collective-permute-start | bytes 1572872 | tf_op jit(solution)/shard_map/ppermute | solution.py:220
  119.9 17.8 %collective-permute-start.35 = (bf16[256,1024]{1,0:T(8,128)(2,1)S(1)}, bf16[256,1024]{1,0:T(8,128)(2,1)S(1)}, u32[]{:S(2)}, u32[]{:S(2)}) collective-permute-start(bf16[256,1024]{1,0:T(8,128)(2,1)S(1)} %collective-permute-done.11.refs_0_.refs_3_), channel_id=1, source_target_pairs={{0,4},{4,0},{8,12},{12,8},{16,20},{20,16},{24,28},{28,24},{1,5},{5... | collective-permute-start | bytes 1572872 | tf_op jit(solution)/shard_map/ppermute | solution.py:220
  119.9 17.8 %collective-permute-start.33 = (bf16[256,1024]{1,0:T(8,128)(2,1)S(1)}, bf16[256,1024]{1,0:T(8,128)(2,1)S(1)}, u32[]{:S(2)}, u32[]{:S(2)}) collective-permute-start(bf16[256,1024]{1,0:T(8,128)(2,1)S(1)} %collective-permute-done.8.refs_0_.refs_1_), channel_id=1, source_target_pairs={{0,4},{4,0},{8,12},{12,8},{16,20},{20,16},{24,28},{28,24},{1,5},{5... | collective-permute-start | bytes 1572872 | tf_op jit(solution)/shard_map/ppermute | solution.py:220
  131.1 34.7 %collective-permute-start.14 = (bf16[128,1536]{1,0:T(8,128)(2,1)S(1)}, bf16[128,1536]{1,0:T(8,128)(2,1)S(1)}, u32[]{:S(2)}, u32[]{:S(2)}) collective-permute-start(bf16[128,1536]{1,0:T(8,128)(2,1)S(1)} %get-tuple-element.27), channel_id=1, source_target_pairs={{0,16},{4,20},{8,24},{12,28},{16,0},{20,4},{24,8},{28,12},{1,17},{... | collective-permute-start | bytes 1179656 | tf_op jit(solution)/shard_map/ppermute | solution.py:217
  133.2 33.3 %collective-permute-start.26 = (bf16[256,1024]{1,0:T(8,128)(2,1)S(1)}, bf16[256,1024]{1,0:T(8,128)(2,1)S(1)}, u32[]{:S(2)}, u32[]{:S(2)}) collective-permute-start(bf16[256,1024]{1,0:T(8,128)(2,1)S(1)} %get-tuple-element.33), channel_id=1, source_target_pairs={{0,1},{3,2},{4,5},{7,6},{8,9},{11,10},{12,13},{15,14},{16,17},{19,... | collective-permute-start | bytes 1572872 | tf_op jit(solution)/shard_map/ppermute | solution.py:232
  162.2 14.4 %collective-permute-start.16 = (bf16[128,1536]{1,0:T(8,128)(2,1)S(1)}, bf16[128,1536]{1,0:T(8,128)(2,1)S(1)}, u32[]{:S(2)}, u32[]{:S(2)}) collective-permute-start(bf16[128,1536]{1,0:T(8,128)(2,1)S(1)} %get-tuple-element.28), channel_id=1, source_target_pairs={{0,16},{4,20},{8,24},{12,28},{16,0},{20,4},{24,8},{28,12},{1,17},{... | collective-permute-start | bytes 1179656 | tf_op jit(solution)/shard_map/ppermute | solution.py:217
  163.8 12.0 %collective-permute-start.12 = (bf16[128,1536]{1,0:T(8,128)(2,1)S(1)}, bf16[128,1536]{1,0:T(8,128)(2,1)S(1)}, u32[]{:S(2)}, u32[]{:S(2)}) collective-permute-start(bf16[128,1536]{1,0:T(8,128)(2,1)S(1)} %get-tuple-element.24), channel_id=1, source_target_pairs={{0,8},{4,12},{8,0},{12,4},{16,24},{20,28},{24,16},{28,20},{1,9},{5... | collective-permute-start | bytes 1179656 | tf_op jit(solution)/shard_map/ppermute | solution.py:217
  164.3 32.6 %collective-permute-start.10 = (bf16[128,1536]{1,0:T(8,128)(2,1)S(1)}, bf16[128,1536]{1,0:T(8,128)(2,1)S(1)}, u32[]{:S(2)}, u32[]{:S(2)}) collective-permute-start(bf16[128,1536]{1,0:T(8,128)(2,1)S(1)} %get-tuple-element.21), channel_id=1, source_target_pairs={{0,8},{4,12},{8,0},{12,4},{16,24},{20,28},{24,16},{28,20},{1,9},{5... | collective-permute-start | bytes 1179656 | tf_op jit(solution)/shard_map/ppermute | solution.py:217
  166.0 25.4 %collective-permute-start.15 = (bf16[128,1536]{1,0:T(8,128)(2,1)S(1)}, bf16[128,1536]{1,0:T(8,128)(2,1)S(1)}, u32[]{:S(2)}, u32[]{:S(2)}) collective-permute-start(bf16[128,1536]{1,0:T(8,128)(2,1)S(1)} %add_convert_fusion.5), channel_id=1, source_target_pairs={{0,8},{4,12},{8,0},{12,4},{16,24},{20,28},{24,16},{28,20},{1,9},{5... | collective-permute-start | bytes 1179656 | tf_op jit(solution)/shard_map/ppermute | solution.py:217
  166.5 25.0 %collective-permute-start.29 = (bf16[256,1024]{1,0:T(8,128)(2,1)S(1)}, bf16[256,1024]{1,0:T(8,128)(2,1)S(1)}, u32[]{:S(2)}, u32[]{:S(2)}) collective-permute-start(bf16[256,1024]{1,0:T(8,128)(2,1)S(1)} %get-tuple-element.34), channel_id=1, source_target_pairs={{0,1},{3,2},{4,5},{7,6},{8,9},{11,10},{12,13},{15,14},{16,17},{19,... | collective-permute-start | bytes 1572872 | tf_op jit(solution)/shard_map/ppermute | solution.py:232
  175.8 15.7 %collective-permute-start.27 = (bf16[256,1024]{1,0:T(8,128)(2,1)S(1)}, bf16[256,1024]{1,0:T(8,128)(2,1)S(1)}, u32[]{:S(2)}, u32[]{:S(2)}) collective-permute-start(bf16[256,1024]{1,0:T(8,128)(2,1)S(1)} %add_convert_fusion.3), channel_id=1, source_target_pairs={{2,1},{1,2},{6,5},{5,6},{10,9},{9,10},{14,13},{13,14},{18,17},{17,... | collective-permute-start | bytes 1572872 | tf_op jit(solution)/shard_map/ppermute | solution.py:232
  176.6 20.4 %collective-permute-start.13 = (bf16[128,1536]{1,0:T(8,128)(2,1)S(1)}, bf16[128,1536]{1,0:T(8,128)(2,1)S(1)}, u32[]{:S(2)}, u32[]{:S(2)}) collective-permute-start(bf16[128,1536]{1,0:T(8,128)(2,1)S(1)} %add_convert_fusion.7), channel_id=1, source_target_pairs={{0,16},{4,20},{8,24},{12,28},{16,0},{20,4},{24,8},{28,12},{1,17},{... | collective-permute-start | bytes 1179656 | tf_op jit(solution)/shard_map/ppermute | solution.py:217
  194.3 13.5 %collective-permute-start.28 = (bf16[256,1024]{1,0:T(8,128)(2,1)S(1)}, bf16[256,1024]{1,0:T(8,128)(2,1)S(1)}, u32[]{:S(2)}, u32[]{:S(2)}) collective-permute-start(bf16[256,1024]{1,0:T(8,128)(2,1)S(1)} %get-tuple-element.31), channel_id=1, source_target_pairs={{1,0},{0,1},{3,2},{2,3},{5,4},{4,5},{7,6},{6,7},{9,8},{8,9},{11,10... | collective-permute-start | bytes 1572872 | tf_op jit(solution)/shard_map/ppermute | solution.py:232
  (35 other events, 364.1 us)
where the time goes:
time: 210 us; the launch traced here: 209 us
  waiting for transfers between devices  88.6 us (42%)
  Pallas kernels  52.6 us (25%)
  starting transfers between devices  41 us (20%)
  local copies, waits for them, and re-layouts  17.6 us (8%)
  other arithmetic  8.35 us (4%)
    ppermute x20, waiting for transfers between devices, across(): return lax.ppermute(value, 'loop', pairs)  67.5 us
    ppermute x20, starting transfers between devices, across(): return lax.ppermute(value, 'loop', pairs)  22.5 us
    ppermute x10, waiting for transfers between devices, along(): return lax.ppermute(value, 'tp', pairs)  20 us
    pallas_call x3, Pallas kernels, input_terms(): pl.pallas_call(functools.partial(input_kernel, blocks=len(blocks), tile=t...  19.1 us
    unnamed x50, local copies, waits for them, and re-layouts  16.5 us
    ppermute x10, starting transfers between devices, along(): return lax.ppermute(value, 'tp', pairs)  16.3 us
    pallas_call x1, Pallas kernels, weight_gradient(): pl.pallas_call(functools.partial(weight_kernel, blocks=len(blocks), grads...  14.9 us
    pallas_call x2, Pallas kernels, project_parts(): pl.pallas_call(functools.partial(project_kernel, blocks=len(blocks)), gri...  14.8 us
  transfers between devices with their start and end apart: 43, of which 14 were waited for; matrix products, arithmetic and copies ran while one was open for 4% of the time, Pallas kernels for 25%

commit v1 on v0

--- a/solution.py
+++ b/solution.py
@@ -11,24 +11,45 @@
 
 BF16 = jnp.bfloat16
 F32 = jnp.float32
-
-
-def kind_kernel(kinds_of_loops, dest, out, *, capacity):
+KIND_ROWS = 8
+PROJECT_TILE = 512
+WEIGHT_TILE = 256
+
+
+def pack_kernel(kinds_of_loops, dest, grads, *outs, capacity):
     slots = dest[...]
     found = jnp.full(slots.shape, kinds_of_loops[0], jnp.int32)
     for loop_index in range(1, kinds_of_loops.shape[0]):
         found = jnp.where(slots >= loop_index * capacity, kinds_of_loops[loop_index], found)
-    out[...] = found
-
-
-def modality_of(dest_row, loop_modality, capacity):
+    cut = slots.shape[1] // len(outs)
+    for part, out in enumerate(outs):
+        extra = out.shape[0] - cut
+        kind = found[:, part * cut:(part + 1) * cut].astype(F32).astype(BF16)
+        out[:cut] = grads[part * cut:(part + 1) * cut]
+        out[cut:] = jnp.zeros((extra, out.shape[1]), BF16)
+        out[cut:, :cut] = jnp.broadcast_to(kind, (extra, cut))
+
+
+def packed_grads(out_grad, dest_row, loop_modality, capacity):
+    rows, columns = out_grad.shape
     slots = dest_row.reshape(1, -1)
-    return pl.pallas_call(
-        functools.partial(kind_kernel, capacity=capacity),
-        out_shape=jax.ShapeDtypeStruct(slots.shape, jnp.int32),
-        in_specs=[pl.BlockSpec(memory_space=pltpu.SMEM), pl.BlockSpec(memory_space=pltpu.VMEM)],
-        out_specs=pl.BlockSpec(memory_space=pltpu.VMEM),
-    )(loop_modality, slots)
+    vmem = pl.BlockSpec(memory_space=pltpu.VMEM)
+    return pl.pallas_call(
+        functools.partial(pack_kernel, capacity=capacity),
+        out_shape=[jax.ShapeDtypeStruct((rows // 2 + KIND_ROWS, columns), BF16)] * 2,
+        in_specs=[pl.BlockSpec(memory_space=pltpu.SMEM), vmem, vmem],
+        out_specs=[vmem, vmem],
+        compiler_params=limit(8),
+    )(loop_modality, slots, out_grad)
+
+
+def kinds_in(refs):
+    return jnp.concatenate([ref[:1].astype(F32) for ref in refs], axis=1)
+
+
+def kind_spec(half_block):
+    cut = half_block.shape[0] - KIND_ROWS
+    return pl.BlockSpec((KIND_ROWS, cut), lambda *_: (cut // KIND_ROWS, 0))
 
 
 def pick(kind, products):
@@ -53,8 +74,10 @@
     return pltpu.CompilerParams(vmem_limit_bytes=mebibytes << 20)
 
 
-def input_kernel(core, kind, own_weight, other_weight, *refs, blocks, tile):
-    rhs = jnp.concatenate([ref[...] for ref in refs[:blocks]], axis=0)
+def input_kernel(core, own_weight, other_weight, *refs, blocks, tile):
+    cut = refs[0].shape[0] - KIND_ROWS
+    rhs = jnp.concatenate([ref[:cut] for ref in refs[:blocks]], axis=0)
+    kind = kinds_in([ref[cut:, :cut] for ref in refs[:blocks]])
     outs = refs[blocks:]
     half = outs[0].shape[1] // 2
     kinds, _, columns = own_weight.shape
@@ -64,13 +87,13 @@
             preferred_element_type=F32,
         )
         products = [product[index * tile:(index + 1) * tile] for index in range(kinds)]
-        chosen = pick(kind[...], products).astype(BF16).T
+        chosen = pick(kind, products).astype(BF16).T
         at = pl.multiple_of(side * half + pl.program_id(0) * tile, tile)
         for out, part in split_rows(chosen, outs):
             out[:, pl.ds(at, tile)] = part
 
 
-def input_terms(core, kind, blocks, sizes, own_weight, other_weight):
+def input_terms(core, blocks, sizes, own_weight, other_weight):
     kinds, half, columns = own_weight.shape
     tile = min(half, 256)
     weight_spec = pl.BlockSpec((kinds, tile, columns), lambda step, core: (0, step, 0))
@@ -79,82 +102,84 @@
         grid_spec=pltpu.PrefetchScalarGridSpec(
             num_scalar_prefetch=1,
             grid=(half // tile,),
-            in_specs=[whole(kind.shape), weight_spec, weight_spec] + [whole(block.shape) for block in blocks],
+            in_specs=[weight_spec, weight_spec] + [whole(block.shape) for block in blocks],
             out_specs=[whole((size, 2 * half)) for size in sizes],
         ),
         out_shape=[jax.ShapeDtypeStruct((size, 2 * half), BF16) for size in sizes],
         compiler_params=limit(28),
-    )(core, kind, own_weight, other_weight, *blocks)
-
-
-def project_kernel(core, kind, own_weight, other_weight, *refs, blocks):
+    )(core, own_weight, other_weight, *blocks)
+
+
+def project_kernel(core, own_weight, other_weight, *refs, blocks, halves):
     _, half, tile = own_weight.shape
     own_at = pl.multiple_of(core[0] * half, half)
     other_at = pl.multiple_of((1 - core[0]) * half, half)
     own = jnp.concatenate([ref[:, pl.ds(own_at, half)] for ref in refs[:blocks]], axis=0)
     other = jnp.concatenate([ref[:, pl.ds(other_at, half)] for ref in refs[:blocks]], axis=0)
-    row_kind = jnp.broadcast_to(kind[...], (tile, own.shape[0])).T
+    kind = kinds_in([ref[...] for ref in refs[blocks:blocks + halves]])
+    row_kind = jnp.broadcast_to(kind, (tile, kind.shape[1])).T
     products = [
         jnp.dot(own, own_weight[index], preferred_element_type=F32)
         + jnp.dot(other, other_weight[index], preferred_element_type=F32)
         for index in range(own_weight.shape[0])
     ]
     chosen = pick(row_kind, products).astype(BF16)
-    for out, part in split_rows(chosen, refs[blocks:]):
+    for out, part in split_rows(chosen, refs[blocks + halves:]):
         out[...] = part
 
 
-def project_parts(core, kind, blocks, sizes, own_weight, other_weight):
+def project_parts(core, blocks, half_blocks, sizes, own_weight, other_weight):
     kinds, half, columns = own_weight.shape
-    tile = math.gcd(columns, 512)
+    tile = math.gcd(columns, PROJECT_TILE)
     weight_spec = pl.BlockSpec((kinds, half, tile), lambda step, core: (0, 0, step))
     return pl.pallas_call(
-        functools.partial(project_kernel, blocks=len(blocks)),
+        functools.partial(project_kernel, blocks=len(blocks), halves=len(half_blocks)),
         grid_spec=pltpu.PrefetchScalarGridSpec(
             num_scalar_prefetch=1,
             grid=(columns // tile,),
-            in_specs=[whole(kind.shape), weight_spec, weight_spec] + [whole(block.shape) for block in blocks],
+            in_specs=[weight_spec, weight_spec]
+            + [whole(block.shape) for block in blocks]
+            + [kind_spec(block) for block in half_blocks],
             out_specs=[pl.BlockSpec((size, tile), lambda step, core: (0, step)) for size in sizes],
         ),
         out_shape=[jax.ShapeDtypeStruct((size, columns), BF16) for size in sizes],
         compiler_params=limit(28),
-    )(core, kind, own_weight, other_weight, *blocks)
+    )(core, own_weight, other_weight, *blocks, *half_blocks)
 
 
 def choose_kernel(wanted, *refs, sources):
-    outs = refs[sources:]
+    outs, done = refs[sources:-1], refs[-1]
     for place, out in enumerate(outs):
         for index, source in enumerate(refs[:sources]):
             @pl.when(wanted[place] == index)
-            def _(out=out, source=source):
-                out[...] = source[...]
+            def _(place=place, out=out, source=source):
+                pltpu.make_async_copy(source, out, done.at[place]).start()
+    for place, out in enumerate(outs):
+        pltpu.make_async_copy(refs[0], out, done.at[place]).wait()
 
 
 def choose(wanted, sources, count):
-    rows, columns = sources[0].shape
-    step_rows = rows // 4
-    spec = pl.BlockSpec((step_rows, columns), lambda step, wanted: (step, 0))
+    any_space = pl.BlockSpec(memory_space=pl.ANY)
     return pl.pallas_call(
         functools.partial(choose_kernel, sources=len(sources)),
-        grid_spec=pltpu.PrefetchScalarGridSpec(
-            num_scalar_prefetch=1,
-            grid=(4,),
-            in_specs=[spec] * len(sources),
-            out_specs=[spec] * count,
-        ),
-        out_shape=[jax.ShapeDtypeStruct((rows, columns), sources[0].dtype)] * count,
-        compiler_params=limit(16),
+        in_specs=[pl.BlockSpec(memory_space=pltpu.SMEM)] + [any_space] * len(sources),
+        out_specs=[any_space] * count,
+        out_shape=[jax.ShapeDtypeStruct(sources[0].shape, sources[0].dtype)] * count,
+        scratch_shapes=[pltpu.SemaphoreType.DMA((count,))],
+        compiler_params=limit(4),
     )(wanted, *sources)
 
 
-def weight_kernel(core, kind, *refs, blocks, grads, scale):
+def weight_kernel(core, *refs, blocks, grads, scale):
     rows = refs[:blocks]
-    cotangents = refs[blocks:blocks + grads]
-    out, turned = refs[blocks + grads:]
+    columns_of = refs[blocks:blocks + grads]
+    kind_rows = refs[blocks + grads:blocks + 2 * grads]
+    out, turned = refs[blocks + 2 * grads:]
     kinds, half, _ = out.shape
 
     @pl.when(pl.program_id(0) == 0)
     def _():
+        kind = kinds_in([ref[...] for ref in kind_rows])
         start = 0
         for ref in rows:
             count = ref.shape[0]
@@ -164,31 +189,32 @@
                 turned[which, :, start:start + count] = jnp.where(own_kind == which, part, 0)
             start += count
 
-    columns = jnp.concatenate([ref[...] for ref in cotangents], axis=0)
+    columns = jnp.concatenate([ref[...] for ref in columns_of], axis=0)
     for which in range(kinds):
         total = jnp.dot(turned[which], columns, preferred_element_type=F32)
         out[which] = (total * scale).astype(BF16)
 
 
-def weight_gradient(core, kind, blocks, grads, kinds, scale):
-    half = blocks[0].shape[1] // 2
-    columns = grads[0].shape[1]
-    tile = min(columns, 256)
-    rows = kind.shape[1]
-    return pl.pallas_call(
-        functools.partial(weight_kernel, blocks=len(blocks), grads=len(grads), scale=scale),
+def weight_gradient(core, blocks, half_blocks, kinds, scale):
+    rows, features = blocks[0].shape
+    half = features // 2
+    columns = half_blocks[0].shape[1]
+    cut = half_blocks[0].shape[0] - KIND_ROWS
+    tile = math.gcd(columns, WEIGHT_TILE)
+    return pl.pallas_call(
+        functools.partial(weight_kernel, blocks=len(blocks), grads=len(half_blocks), scale=scale),
         grid_spec=pltpu.PrefetchScalarGridSpec(
             num_scalar_prefetch=1,
             grid=(columns // tile,),
-            in_specs=[whole(kind.shape)]
-            + [whole(block.shape) for block in blocks]
-            + [pl.BlockSpec((block.shape[0], tile), lambda step, core: (0, step)) for block in grads],
+            in_specs=[whole(block.shape) for block in blocks]
+            + [pl.BlockSpec((cut, tile), lambda step, core: (0, step)) for _ in half_blocks]
+            + [kind_spec(block) for block in half_blocks],
             out_specs=pl.BlockSpec((kinds, half, tile), lambda step, core: (0, 0, step)),
-            scratch_shapes=[pltpu.VMEM((kinds, half, rows), BF16)],
+            scratch_shapes=[pltpu.VMEM((kinds, half, rows * len(blocks)), BF16)],
         ),
         out_shape=jax.ShapeDtypeStruct((kinds, half, columns), BF16),
         compiler_params=limit(36),
-    )(core, kind, *blocks, *grads)
+    )(core, *blocks, *half_blocks, *half_blocks)
 
 
 def low_high(offset):
@@ -242,7 +268,7 @@
             if pairs:
                 came[parity, stage] = along(came[1 - parity, stage - 1], pairs)
 
-    own_grad = [out_grad[:cut], out_grad[cut:]]
+    own_grad = packed_grads(out_grad, dest_row, loop_modality, capacity)
     grads = {0: own_grad}
     for bit in bits:
         grads[bit] = [None, None]
@@ -254,20 +280,14 @@
         low, high = low_high(offset)
         grads[offset] = [across(grads[offset ^ low][0], low), across(grads[offset ^ high][1], high)]
 
-    own_kind = modality_of(dest_row, loop_modality, capacity)
-    kind = own_kind
-    for bit in bits:
-        kind = jnp.concatenate([kind, across(kind, bit)], axis=0)
-    other_kind = sibling(kind)
-    kind_of = [own_kind] + [kind[offset:offset + 1] for offset in range(1, chip_count)]
-
-    def group_kind(group):
-        return jnp.concatenate([kind_of[offset] for offset in group], axis=1)
+    def halves_of(group):
+        return [part for offset in group for part in grads[offset]]
 
     arrived = {}
     for group in ([0], bits, several):
-        blocks = [out_grad] if group == [0] else [part for offset in group for part in grads[offset]]
-        made = input_terms(core, group_kind(group), blocks, [row_count] * len(group), qkv_weight, other_weight)
+        made = input_terms(
+            core, halves_of(group), [row_count] * len(group), qkv_weight, other_weight
+        )
         for offset, term in zip(group, made):
             arrived[offset] = across(term, offset) if offset else term
     all_terms = [arrived[offset] for offset in range(chip_count)]
@@ -305,12 +325,15 @@
                 index = jnp.where(where == level + stage * facing[parity], number, index)
         wanted.append(index)
     sends = choose(jnp.stack(wanted), sources, chip_count)
-    rows = {offset: across(sends[offset], offset) if offset else sends[offset] for offset in range(chip_count)}
+    rows = {
+        offset: across(sends[offset], offset) if offset else sends[offset]
+        for offset in range(chip_count)
+    }
 
     parts = {}
-    for group in (several, bits + [0]):
+    for group in (several, bits, [0]):
         made = project_parts(
-            core, group_kind(group), [rows[offset] for offset in group],
+            core, [rows[offset] for offset in group], halves_of(group),
             [cut] * (2 * len(group)), qkv_weight, other_weight,
         )
         for place, offset in enumerate(group):
@@ -328,10 +351,9 @@
 
     near = [rows[offset] for offset in range(chip_count)]
     far = [sibling(block) for block in near]
-    near_grads = [out_grad] + [part for offset in range(1, chip_count) for part in grads[offset]]
+    near_grads = halves_of(range(chip_count))
     far_grads = [sibling(block) for block in near_grads]
-    all_kind = jnp.concatenate([kind.reshape(1, -1), other_kind.reshape(1, -1)], axis=1)
-    weight_grad = weight_gradient(core, all_kind, near + far, near_grads + far_grads, kinds, grad_scale)
+    weight_grad = weight_gradient(core, near + far, near_grads + far_grads, kinds, grad_scale)
     return projected, input_grad, weight_grad
 
 

time: 210 us -> 242 us (1.15)
  starting transfers between devices: 41 us -> 59.1 us
  Pallas kernels: 52.6 us -> 69.8 us
  waiting for transfers between devices: 88.6 us -> 79.9 us
  local copies, waits for them, and re-layouts: 17.6 us -> 22.8 us
    pallas_call x4 -> x5, Pallas kernels: 18.7 us -> 36.8 us  [the longest x3 18.6 us: project_parts(): pl.pallas_call(functools.partial(project_kernel, blocks=len(blocks), halv...]
    ppermute x20 -> x18, starting transfers between devices: 22.5 us -> 40.4 us  [across(): return lax.ppermute(value, 'loop', pairs)]
    ppermute x20 -> x18, waiting for transfers between devices: 67.5 us -> 51.6 us  [across(): return lax.ppermute(value, 'loop', pairs)]
    ppermute x10, waiting for transfers between devices: 20 us -> 27.6 us  [along(): return lax.ppermute(value, 'tp', pairs)]
    unnamed x50 -> x72, local copies, waits for them, and re-layouts: 16.5 us -> 22.8 us
  transfers between devices with their start and end apart: 43 -> 41, of which waited for: 14 -> 15; matrix products, arithmetic and copies ran while one was open for 4% -> 2% of each run, Pallas kernels for 25% -> 29%
where the time goes in v1:
time: 242 us; the launch traced here: 240 us
  waiting for transfers between devices  79.9 us (33%)
  Pallas kernels  69.8 us (29%)
  starting transfers between devices  59.1 us (24%)
  local copies, waits for them, and re-layouts  22.8 us (9%)
  other arithmetic  7.35 us (3%)
    ppermute x18, waiting for transfers between devices, across(): return lax.ppermute(value, 'loop', pairs)  51.6 us
    ppermute x18, starting transfers between devices, across(): return lax.ppermute(value, 'loop', pairs)  40.4 us
    ppermute x10, waiting for transfers between devices, along(): return lax.ppermute(value, 'tp', pairs)  27.6 us
    unnamed x72, local copies, waits for them, and re-layouts  22.8 us
    pallas_call x3, Pallas kernels, project_parts(): pl.pallas_call(functools.partial(project_kernel, blocks=len(blocks), halv...  18.6 us
    ppermute x10, starting transfers between devices, along(): return lax.ppermute(value, 'tp', pairs)  18.1 us
    pallas_call x1, Pallas kernels, choose(): pl.pallas_call(functools.partial(choose_kernel, sources=len(sources)), in...  17.6 us
    pallas_call x3, Pallas kernels, input_terms(): pl.pallas_call(functools.partial(input_kernel, blocks=len(blocks), tile=t...  17 us
  transfers between devices with their start and end apart: 41, of which 15 were waited for; matrix products, arithmetic and copies ran while one was open for 2% of the time, Pallas kernels for 29%

profile of v1, /device:TPU:0, one launch (start us, length us, event | category | flops | bytes accessed | tf_op | source)
XLA Modules:
  0.0 240.0 jit_solution(10994367285799393710)
XLA Ops:
  4.3 3.0 %collective-permute-start.10 = (bf16[136,1536]{1,0:T(8,128)(2,1)S(1)}, bf16[136,1536]{1,0:T(8,128)(2,1)S(1)}, u32[]{:S(2)}, u32[]{:S(2)}) collective-permute-start(bf16[136,1536]{1,0:T(8,128)(2,1)S(1)} %get-tuple-element.20.refs_1_.refs_0_.refs_8_.refs_24_), channel_id=1, source_target_pairs={{0,16},{4,20},{8,24},{12,28},{16,0},{20,4},{24,8},{28,12},{1,17},{... | collective-permute-start | bytes 1253384 | tf_op jit(solution)/shard_map/ppermute | solution.py:243
  10.3 2.9 %collective-permute-start.1 = (bf16[256,1024]{1,0:T(8,128)(2,1)}, bf16[256,1024]{1,0:T(8,128)(2,1)S(1)}, u32[]{:S(2)}, u32[]{:S(2)}) collective-permute-start(bf16[256,1024]{1,0:T(8,128)(2,1)} %refs_0_.1), channel_id=1, source_target_pairs={{0,1},{1,0},{2,3},{3,2},{4,5},{5,4},{6,7},{7,6},{8,9},{9,8},{10,11... | collective-permute-start | bytes 1572872 | tf_op jit(solution)/shard_map/ppermute | solution.py:258
  13.2 4.0 %collective-permute-done.10.refs_4_.refs_2_.refs_12_.refs_28_ = bf16[136,1536]{1,0:T(8,128)(2,1)S(1)} collective-permute-done((bf16[136,1536]{1,0:T(8,128)(2,1)S(1)}, bf16[136,1536]{1,0:T(8,128)(2,1)S(1)}, u32[]{:S(2)}, u32[]{:S(2)}) %collective-permute-start.10) | collective-permute-done | bytes 417824 | tf_op jit(solution)/shard_map/ppermute | solution.py:243
  17.2 1.7 collective-permute-start.11
  22.7 3.0 %collective-permute-done.1.refs_1_ = bf16[256,1024]{1,0:T(8,128)(2,1)S(1)} collective-permute-done((bf16[256,1024]{1,0:T(8,128)(2,1)}, bf16[256,1024]{1,0:T(8,128)(2,1)S(1)}, u32[]{:S(2)}, u32[]{:S(2)}) %collective-permute-start.1) | collective-permute-done | bytes 524320 | tf_op jit(solution)/shard_map/ppermute | solution.py:258
  34.3 6.0 %collective-permute-done.14.refs_1_.refs_0_.refs_14_.refs_30_ = bf16[136,1536]{1,0:T(8,128)(2,1)S(1)} collective-permute-done((bf16[136,1536]{1,0:T(8,128)(2,1)S(1)}, bf16[136,1536]{1,0:T(8,128)(2,1)S(1)}, u32[]{:S(2)}, u32[]{:S(2)}) %collective-permute-start.14) | collective-permute-done | bytes 417824 | tf_op jit(solution)/shard_map/ppermute | solution.py:243
  42.6 8.4 %collective-permute-done.15.refs_2_.refs_1_.refs_15_.refs_31_ = bf16[136,1536]{1,0:T(8,128)(2,1)S(1)} collective-permute-done((bf16[136,1536]{1,0:T(8,128)(2,1)S(1)}, bf16[136,1536]{1,0:T(8,128)(2,1)S(1)}, u32[]{:S(2)}, u32[]{:S(2)}) %collective-permute-start.15) | collective-permute-done | bytes 417824 | tf_op jit(solution)/shard_map/ppermute | solution.py:243
  51.0 4.0 %collective-permute-done.3.refs_3_ = bf16[256,1024]{1,0:T(8,128)(2,1)} collective-permute-done((bf16[256,1024]{1,0:T(8,128)(2,1)}, bf16[256,1024]{1,0:T(8,128)(2,1)}, u32[]{:S(2)}, u32[]{:S(2)}) %collective-permute-start.3) | collective-permute-done | bytes 524320 | tf_op jit(solution)/shard_map/ppermute | solution.py:258
  55.0 11.1 %collective-permute-done.5.refs_5_ = bf16[256,1024]{1,0:T(8,128)(2,1)} collective-permute-done((bf16[256,1024]{1,0:T(8,128)(2,1)}, bf16[256,1024]{1,0:T(8,128)(2,1)}, u32[]{:S(2)}, u32[]{:S(2)}) %collective-permute-start.5) | collective-permute-done | bytes 524320 | tf_op jit(solution)/shard_map/ppermute | solution.py:258
  68.2 17.6 %shard_map.76 = (bf16[256,1024]{1,0:T(8,128)(2,1)}, bf16[256,1024]{1,0:T(8,128)(2,1)}, bf16[256,1024]{1,0:T(8,128)(2,1)}, bf16[256,1024]{1,0:T(8,128)(2,1)S(1)}) custom-call(s32[4]{0:T(128)S(1)} %pad_add_fusion.wanted, bf16[256,1024]{1,0:T(8,128)(2,1)S(1)} %copy-done.15, bf16[256,1024]{1,0:T(8,128)(2,1)S(1)} %copy-done.17, ...), custom_call_target="tpu_custom_call" | custom-call | tf_op jit(solution)/shard_map/pallas_call | solution.py:163
  87.1 16.4 %collective-permute-start.7 = (bf16[256,1024]{1,0:T(8,128)(2,1)}, bf16[256,1024]{1,0:T(8,128)(2,1)}, u32[]{:S(2)}, u32[]{:S(2)}) collective-permute-start(bf16[256,1024]{1,0:T(8,128)(2,1)} %get-tuple-element.24), channel_id=1, source_target_pairs={{0,16},{4,20},{8,24},{12,28},{16,0},{20,4},{24,8},{28,12},{1,17},{... | collective-permute-start | bytes 1572872 | tf_op jit(solution)/shard_map/ppermute | solution.py:243
  103.5 2.3 copy-done
  105.8 7.3 %shard_map.82 = (bf16[256,1024]{1,0:T(8,128)(2,1)S(1)}, bf16[256,1024]{1,0:T(8,128)(2,1)S(1)}) custom-call(s32[1]{0:T(128)} %bitcast.core, bf16[3,512,1536]{2,1,0:T(8,128)(2,1)S(1)} %copy-done, bf16[3,512,1536]{2,1,0:T(8,128)(2,1)} %collective-permute-done.other_weight, bf16[136,1536]{1,0:T(8,128)(2,1)S(1)} %collective-permute-done.8.refs_2_.refs_0_.refs_10_.refs_26_, ...), custom_call_target="tpu_custom_call" | custom-call | tf_op jit(solution)/shard_map/pallas_call | solution.py:100
  114.1 2.0 collective-permute-start.22
  116.7 4.9 %shard_map.81 = bf16[256,1024]{1,0:T(8,128)(2,1)S(1)} custom-call(s32[1]{0:T(128)} %bitcast.core, bf16[3,512,1536]{2,1,0:T(8,128)(2,1)S(1)} %copy-done, bf16[3,512,1536]{2,1,0:T(8,128)(2,1)} %collective-permute-done.other_weight, bf16[136,1536]{1,0:T(8,128)(2,1)S(1)} %collective-permute-done.14.refs_1_.refs_0_.refs_14_.refs_30_, ...), custom_call_target="tpu_custom_call" | custom-call | tf_op jit(solution)/shard_map/pallas_call | solution.py:100
  122.6 4.6 %collective-permute-done.7.refs_1_.refs_2_ = bf16[256,1024]{1,0:T(8,128)(2,1)} collective-permute-done((bf16[256,1024]{1,0:T(8,128)(2,1)}, bf16[256,1024]{1,0:T(8,128)(2,1)}, u32[]{:S(2)}, u32[]{:S(2)}) %collective-permute-start.7) | collective-permute-done | bytes 524320 | tf_op jit(solution)/shard_map/ppermute | solution.py:243
  127.2 1.8 collective-permute-done.13.refs_0_.refs_3_
  129.0 19.9 %collective-permute-done.22 = bf16[256,1024]{1,0:T(8,128)(2,1)S(1)} collective-permute-done((bf16[256,1024]{1,0:T(8,128)(2,1)S(1)}, bf16[256,1024]{1,0:T(8,128)(2,1)S(1)}, u32[]{:S(2)}, u32[]{:S(2)}) %collective-permute-start.22) | collective-permute-done | bytes 524320 | tf_op jit(solution)/shard_map/ppermute | solution.py:243
  149.8 5.8 %shard_map.80 = (bf16[128,1536]{1,0:T(8,128)(2,1)}, bf16[128,1536]{1,0:T(8,128)(2,1)S(1)}) custom-call(s32[1]{0:T(128)} %bitcast.core, bf16[3,512,1536]{2,1,0:T(8,128)(2,1)S(1)} %copy-done, bf16[3,512,1536]{2,1,0:T(8,128)(2,1)} %collective-permute-done.other_weight, bf16[256,1024]{1,0:T(8,128)(2,1)} %collective-permute-done.13.refs_0_.refs_3_, ...), custom_call_target="tpu_custom_call" | custom-call | tf_op jit(solution)/shard_map/pallas_call | solution.py:135
  158.7 2.3 copy-done.1
  161.0 4.9 %shard_map.83 = bf16[256,1024]{1,0:T(8,128)(2,1)S(1)} custom-call(s32[1]{0:T(128)} %bitcast.core, bf16[3,512,1536]{2,1,0:T(8,128)(2,1)S(1)} %copy-done.1, bf16[3,512,1536]{2,1,0:T(8,128)(2,1)} %collective-permute-done.other_weight, bf16[136,1536]{1,0:T(8,128)(2,1)S(1)} %get-tuple-element.20.refs_1_.refs_0_.refs_8_.refs_24_, ...), custom_call_target="tpu_custom_call" | custom-call | tf_op jit(solution)/shard_map/pallas_call | solution.py:100
  167.2 2.3 collective-permute-start.24
  176.1 16.0 %shard_map.84 = bf16[3,512,1536]{2,1,0:T(8,128)(2,1)} custom-call(s32[1]{0:T(128)} %bitcast.core, bf16[256,1024]{1,0:T(8,128)(2,1)} %get-tuple-element.19.refs_0_, bf16[256,1024]{1,0:T(8,128)(2,1)} %collective-permute-done.6.refs_0_.refs_1_, bf16[256,1024]{1,0:T(8,128)(2,1)} %collective-permute-done.7.refs_1_.refs_2_, ...), custom_call_target="tpu_custom_call" | custom-call | tf_op jit(solution)/shard_map/pallas_call | solution.py:204
  192.0 2.6 %collective-permute-start.18 = (bf16[128,1536]{1,0:T(8,128)(2,1)S(1)}, bf16[128,1536]{1,0:T(8,128)(2,1)S(1)}, u32[]{:S(2)}, u32[]{:S(2)}) collective-permute-start(bf16[128,1536]{1,0:T(8,128)(2,1)S(1)} %copy-done.23), channel_id=1, source_target_pairs={{0,16},{4,20},{8,24},{12,28},{16,0},{20,4},{24,8},{28,12},{1,17},{... | collective-permute-start | bytes 1179656 | tf_op jit(solution)/shard_map/ppermute | solution.py:243
  194.6 7.5 %shard_map.79 = (bf16[128,1536]{1,0:T(8,128)(2,1)S(1)}, bf16[128,1536]{1,0:T(8,128)(2,1)S(1)}, bf16[128,1536]{1,0:T(8,128)(2,1)S(1)}, bf16[128,1536]{1,0:T(8,128)(2,1)S(1)}) custom-call(s32[1]{0:T(128)} %bitcast.core, bf16[3,512,1536]{2,1,0:T(8,128)(2,1)S(1)} %bitcast.7, bf16[3,512,1536]{2,1,0:T(8,128)(2,1)} %collective-permute-done.other_weight, ...), custom_call_target="tpu_custom_call" | custom-call | tf_op jit(solution)/shard_map/pallas_call | solution.py:135
  202.8 5.3 %shard_map.78 = (bf16[128,1536]{1,0:T(8,128)(2,1)S(1)}, bf16[128,1536]{1,0:T(8,128)(2,1)S(1)}) custom-call(s32[1]{0:T(128)} %bitcast.core, bf16[3,512,1536]{2,1,0:T(8,128)(2,1)S(1)} %bitcast.7, bf16[3,512,1536]{2,1,0:T(8,128)(2,1)} %collective-permute-done.other_weight, bf16[256,1024]{1,0:T(8,128)(2,1)} %get-tuple-element.19.refs_0_, ...), custom_call_target="tpu_custom_call" | custom-call | tf_op jit(solution)/shard_map/pallas_call | solution.py:135
  209.2 1.9 collective-permute-start.17
  212.5 1.5 add_convert_fusion.3
  214.8 1.5 collective-permute-start.19
  216.4 5.3 %collective-permute-done.17 = bf16[128,1536]{1,0:T(8,128)(2,1)S(1)} collective-permute-done((bf16[128,1536]{1,0:T(8,128)(2,1)S(1)}, bf16[128,1536]{1,0:T(8,128)(2,1)S(1)}, u32[]{:S(2)}, u32[]{:S(2)}) %collective-permute-start.17) | collective-permute-done | bytes 393248 | tf_op jit(solution)/shard_map/ppermute | solution.py:243
  223.6 4.7 %collective-permute-start.26 = (bf16[256,1024]{1,0:T(8,128)(2,1)S(1)}, bf16[256,1024]{1,0:T(8,128)(2,1)S(1)}, u32[]{:S(2)}, u32[]{:S(2)}) collective-permute-start(bf16[256,1024]{1,0:T(8,128)(2,1)S(1)} %get-tuple-element.35), channel_id=1, source_target_pairs={{1,0},{0,1},{3,2},{2,3},{5,4},{4,5},{7,6},{6,7},{9,8},{8,9},{11,10... | collective-permute-start | bytes 1572872 | tf_op jit(solution)/shard_map/ppermute | solution.py:258
  230.1 8.5 %collective-permute-done.26 = bf16[256,1024]{1,0:T(8,128)(2,1)S(1)} collective-permute-done((bf16[256,1024]{1,0:T(8,128)(2,1)S(1)}, bf16[256,1024]{1,0:T(8,128)(2,1)S(1)}, u32[]{:S(2)}, u32[]{:S(2)}) %collective-permute-start.26) | collective-permute-done | bytes 524320 | tf_op jit(solution)/shard_map/ppermute | solution.py:258
  (142 shorter events, 48.1 us)
Async XLA Ops:
  0.6 86.5 %collective-permute-start = (bf16[3,512,1536]{2,1,0:T(8,128)(2,1)}, bf16[3,512,1536]{2,1,0:T(8,128)(2,1)}, u32[]{:S(2)}, u32[]{:S(2)}) collective-permute-start(bf16[3,512,1536]{2,1,0:T(8,128)(2,1)} %own_weight.11), channel_id=1, source_target_pairs={{0,4},{4,0},{8,12},{12,8},{16,20},{20,16},{24,28},{28,24},{1,5},{5... | collective-permute-start | bytes 14155784 | tf_op jit(solution)/shard_map/ppermute | solution.py:246
  4.3 12.9 %collective-permute-start.10 = (bf16[136,1536]{1,0:T(8,128)(2,1)S(1)}, bf16[136,1536]{1,0:T(8,128)(2,1)S(1)}, u32[]{:S(2)}, u32[]{:S(2)}) collective-permute-start(bf16[136,1536]{1,0:T(8,128)(2,1)S(1)} %get-tuple-element.20.refs_1_.refs_0_.refs_8_.refs_24_), channel_id=1, source_target_pairs={{0,16},{4,20},{8,24},{12,28},{16,0},{20,4},{24,8},{28,12},{1,17},{... | collective-permute-start | bytes 1253384 | tf_op jit(solution)/shard_map/ppermute | solution.py:243
  7.3 11.6 %collective-permute-start.8 = (bf16[136,1536]{1,0:T(8,128)(2,1)S(1)}, bf16[136,1536]{1,0:T(8,128)(2,1)S(1)}, u32[]{:S(2)}, u32[]{:S(2)}) collective-permute-start(bf16[136,1536]{1,0:T(8,128)(2,1)S(1)} %get-tuple-element.20.refs_1_.refs_0_.refs_8_.refs_24_), channel_id=1, source_target_pairs={{0,8},{4,12},{8,0},{12,4},{16,24},{20,28},{24,16},{28,20},{1,9},{5... | collective-permute-start | bytes 1253384 | tf_op jit(solution)/shard_map/ppermute | solution.py:243
  8.8 11.6 %collective-permute-start.34 = (bf16[136,1536]{1,0:T(8,128)(2,1)S(1)}, bf16[136,1536]{1,0:T(8,128)(2,1)S(1)}, u32[]{:S(2)}, u32[]{:S(2)}) collective-permute-start(bf16[136,1536]{1,0:T(8,128)(2,1)S(1)} %get-tuple-element.21.refs_2_.refs_1_.refs_9_.refs_25_), channel_id=1, source_target_pairs={{0,4},{4,0},{8,12},{12,8},{16,20},{20,16},{24,28},{28,24},{1,5},{5... | collective-permute-start | bytes 1253384 | tf_op jit(solution)/shard_map/ppermute | solution.py:246
  10.3 15.4 %collective-permute-start.1 = (bf16[256,1024]{1,0:T(8,128)(2,1)}, bf16[256,1024]{1,0:T(8,128)(2,1)S(1)}, u32[]{:S(2)}, u32[]{:S(2)}) collective-permute-start(bf16[256,1024]{1,0:T(8,128)(2,1)} %refs_0_.1), channel_id=1, source_target_pairs={{0,1},{1,0},{2,3},{3,2},{4,5},{5,4},{6,7},{7,6},{8,9},{9,8},{10,11... | collective-permute-start | bytes 1572872 | tf_op jit(solution)/shard_map/ppermute | solution.py:258
  17.2 11.1 %collective-permute-start.11 = (bf16[136,1536]{1,0:T(8,128)(2,1)S(1)}, bf16[136,1536]{1,0:T(8,128)(2,1)S(1)}, u32[]{:S(2)}, u32[]{:S(2)}) collective-permute-start(bf16[136,1536]{1,0:T(8,128)(2,1)S(1)} %get-tuple-element.21.refs_2_.refs_1_.refs_9_.refs_25_), channel_id=1, source_target_pairs={{0,16},{4,20},{8,24},{12,28},{16,0},{20,4},{24,8},{28,12},{1,17},{... | collective-permute-start | bytes 1253384 | tf_op jit(solution)/shard_map/ppermute | solution.py:243
  29.5 10.9 %collective-permute-start.14 = (bf16[136,1536]{1,0:T(8,128)(2,1)S(1)}, bf16[136,1536]{1,0:T(8,128)(2,1)S(1)}, u32[]{:S(2)}, u32[]{:S(2)}) collective-permute-start(bf16[136,1536]{1,0:T(8,128)(2,1)S(1)} %collective-permute-done.10.refs_4_.refs_2_.refs_12_.refs_28_), channel_id=1, source_target_pairs={{0,8},{4,12},{8,0},{12,4},{16,24},{20,28},{24,16},{28,20},{1,9},{5... | collective-permute-start | bytes 1253384 | tf_op jit(solution)/shard_map/ppermute | solution.py:243
  31.7 23.2 %collective-permute-start.3 = (bf16[256,1024]{1,0:T(8,128)(2,1)}, bf16[256,1024]{1,0:T(8,128)(2,1)}, u32[]{:S(2)}, u32[]{:S(2)}) collective-permute-start(bf16[256,1024]{1,0:T(8,128)(2,1)} %collective-permute-done.2.refs_2_), channel_id=1, source_target_pairs={{1,0},{2,3},{5,4},{6,7},{9,8},{10,11},{13,12},{14,15},{17,16},{18,... | collective-permute-start | bytes 1572872 | tf_op jit(solution)/shard_map/ppermute | solution.py:258
  33.0 33.0 %collective-permute-start.5 = (bf16[256,1024]{1,0:T(8,128)(2,1)}, bf16[256,1024]{1,0:T(8,128)(2,1)}, u32[]{:S(2)}, u32[]{:S(2)}) collective-permute-start(bf16[256,1024]{1,0:T(8,128)(2,1)} %collective-permute-done.4.refs_4_), channel_id=1, source_target_pairs={{1,0},{2,3},{5,4},{6,7},{9,8},{10,11},{13,12},{14,15},{17,16},{18,... | collective-permute-start | bytes 1572872 | tf_op jit(solution)/shard_map/ppermute | solution.py:258
  42.5 44.1 %collective-permute-start.38 = (bf16[136,1536]{1,0:T(8,128)(2,1)S(1)}, bf16[136,1536]{1,0:T(8,128)(2,1)}, u32[]{:S(2)}, u32[]{:S(2)}) collective-permute-start(bf16[136,1536]{1,0:T(8,128)(2,1)S(1)} %collective-permute-done.11.refs_5_.refs_3_.refs_13_.refs_29_), channel_id=1, source_target_pairs={{0,4},{4,0},{8,12},{12,8},{16,20},{20,16},{24,28},{28,24},{1,5},{5... | collective-permute-start | bytes 1253384 | tf_op jit(solution)/shard_map/ppermute | solution.py:246
  51.0 62.1 %collective-permute-start.36 = (bf16[136,1536]{1,0:T(8,128)(2,1)S(1)}, bf16[136,1536]{1,0:T(8,128)(2,1)}, u32[]{:S(2)}, u32[]{:S(2)}) collective-permute-start(bf16[136,1536]{1,0:T(8,128)(2,1)S(1)} %collective-permute-done.9.refs_3_.refs_1_.refs_11_.refs_27_), channel_id=1, source_target_pairs={{0,4},{4,0},{8,12},{12,8},{16,20},{20,16},{24,28},{28,24},{1,5},{5... | collective-permute-start | bytes 1253384 | tf_op jit(solution)/shard_map/ppermute | solution.py:246
  55.0 59.2 %collective-permute-start.39 = (bf16[136,1536]{1,0:T(8,128)(2,1)S(1)}, bf16[136,1536]{1,0:T(8,128)(2,1)}, u32[]{:S(2)}, u32[]{:S(2)}) collective-permute-start(bf16[136,1536]{1,0:T(8,128)(2,1)S(1)} %collective-permute-done.14.refs_1_.refs_0_.refs_14_.refs_30_), channel_id=1, source_target_pairs={{0,4},{4,0},{8,12},{12,8},{16,20},{20,16},{24,28},{28,24},{1,5},{5... | collective-permute-start | bytes 1253384 | tf_op jit(solution)/shard_map/ppermute | solution.py:246
  66.0 50.1 %collective-permute-start.40 = (bf16[136,1536]{1,0:T(8,128)(2,1)S(1)}, bf16[136,1536]{1,0:T(8,128)(2,1)}, u32[]{:S(2)}, u32[]{:S(2)}) collective-permute-start(bf16[136,1536]{1,0:T(8,128)(2,1)S(1)} %collective-permute-done.15.refs_2_.refs_1_.refs_15_.refs_31_), channel_id=1, source_target_pairs={{0,4},{4,0},{8,12},{12,8},{16,20},{20,16},{24,28},{28,24},{1,5},{5... | collective-permute-start | bytes 1253384 | tf_op jit(solution)/shard_map/ppermute | solution.py:246
  86.6 35.0 %collective-permute-start.6 = (bf16[256,1024]{1,0:T(8,128)(2,1)}, bf16[256,1024]{1,0:T(8,128)(2,1)}, u32[]{:S(2)}, u32[]{:S(2)}) collective-permute-start(bf16[256,1024]{1,0:T(8,128)(2,1)} %get-tuple-element.23), channel_id=1, source_target_pairs={{0,8},{4,12},{8,0},{12,4},{16,24},{20,28},{24,16},{28,20},{1,9},{5... | collective-permute-start | bytes 1572872 | tf_op jit(solution)/shard_map/ppermute | solution.py:243
  87.1 40.1 %collective-permute-start.7 = (bf16[256,1024]{1,0:T(8,128)(2,1)}, bf16[256,1024]{1,0:T(8,128)(2,1)}, u32[]{:S(2)}, u32[]{:S(2)}) collective-permute-start(bf16[256,1024]{1,0:T(8,128)(2,1)} %get-tuple-element.24), channel_id=1, source_target_pairs={{0,16},{4,20},{8,24},{12,28},{16,0},{20,4},{24,8},{28,12},{1,17},{... | collective-permute-start | bytes 1572872 | tf_op jit(solution)/shard_map/ppermute | solution.py:243
  113.1 15.9 %collective-permute-start.13 = (bf16[256,1024]{1,0:T(8,128)(2,1)S(1)}, bf16[256,1024]{1,0:T(8,128)(2,1)}, u32[]{:S(2)}, u32[]{:S(2)}) collective-permute-start(bf16[256,1024]{1,0:T(8,128)(2,1)S(1)} %copy-done.21), channel_id=1, source_target_pairs={{0,24},{4,28},{8,16},{12,20},{16,8},{20,12},{24,0},{28,4},{1,25},{... | collective-permute-start | bytes 1572872 | tf_op jit(solution)/shard_map/ppermute | solution.py:243
  114.1 34.9 %collective-permute-start.22 = (bf16[256,1024]{1,0:T(8,128)(2,1)S(1)}, bf16[256,1024]{1,0:T(8,128)(2,1)S(1)}, u32[]{:S(2)}, u32[]{:S(2)}) collective-permute-start(bf16[256,1024]{1,0:T(8,128)(2,1)S(1)} %get-tuple-element.33), channel_id=1, source_target_pairs={{0,16},{4,20},{8,24},{12,28},{16,0},{20,4},{24,8},{28,12},{1,17},{... | collective-permute-start | bytes 1572872 | tf_op jit(solution)/shard_map/ppermute | solution.py:243
  116.1 32.8 %collective-permute-start.23 = (bf16[256,1024]{1,0:T(8,128)(2,1)S(1)}, bf16[256,1024]{1,0:T(8,128)(2,1)S(1)}, u32[]{:S(2)}, u32[]{:S(2)}) collective-permute-start(bf16[256,1024]{1,0:T(8,128)(2,1)S(1)} %get-tuple-element.34), channel_id=1, source_target_pairs={{0,8},{4,12},{8,0},{12,4},{16,24},{20,28},{24,16},{28,20},{1,9},{5... | collective-permute-start | bytes 1572872 | tf_op jit(solution)/shard_map/ppermute | solution.py:243
  121.6 34.8 %collective-permute-start.21 = (bf16[256,1024]{1,0:T(8,128)(2,1)S(1)}, bf16[256,1024]{1,0:T(8,128)(2,1)S(1)}, u32[]{:S(2)}, u32[]{:S(2)}) collective-permute-start(bf16[256,1024]{1,0:T(8,128)(2,1)S(1)} %shard_map.81), channel_id=1, source_target_pairs={{0,24},{4,28},{8,16},{12,20},{16,8},{20,12},{24,0},{28,4},{1,25},{... | collective-permute-start | bytes 1572872 | tf_op jit(solution)/shard_map/ppermute | solution.py:243
  127.2 40.0 %collective-permute-start.29 = (bf16[256,1024]{1,0:T(8,128)(2,1)}, bf16[256,1024]{1,0:T(8,128)(2,1)}, u32[]{:S(2)}, u32[]{:S(2)}) collective-permute-start(bf16[256,1024]{1,0:T(8,128)(2,1)} %get-tuple-element.19.refs_0_), channel_id=1, source_target_pairs={{0,4},{4,0},{8,12},{12,8},{16,20},{20,16},{24,28},{28,24},{1,5},{5... | collective-permute-start | bytes 1572872 | tf_op jit(solution)/shard_map/ppermute | solution.py:246
  129.0 40.5 %collective-permute-start.30 = (bf16[256,1024]{1,0:T(8,128)(2,1)}, bf16[256,1024]{1,0:T(8,128)(2,1)}, u32[]{:S(2)}, u32[]{:S(2)}) collective-permute-start(bf16[256,1024]{1,0:T(8,128)(2,1)} %collective-permute-done.6.refs_0_.refs_1_), channel_id=1, source_target_pairs={{0,4},{4,0},{8,12},{12,8},{16,20},{20,16},{24,28},{28,24},{1,5},{5... | collective-permute-start | bytes 1572872 | tf_op jit(solution)/shard_map/ppermute | solution.py:246
  149.0 20.5 %collective-permute-start.31 = (bf16[256,1024]{1,0:T(8,128)(2,1)}, bf16[256,1024]{1,0:T(8,128)(2,1)}, u32[]{:S(2)}, u32[]{:S(2)}) collective-permute-start(bf16[256,1024]{1,0:T(8,128)(2,1)} %collective-permute-done.7.refs_1_.refs_2_), channel_id=1, source_target_pairs={{0,4},{4,0},{8,12},{12,8},{16,20},{20,16},{24,28},{28,24},{1,5},{5... | collective-permute-start | bytes 1572872 | tf_op jit(solution)/shard_map/ppermute | solution.py:246
  149.8 19.7 %collective-permute-start.32 = (bf16[256,1024]{1,0:T(8,128)(2,1)}, bf16[256,1024]{1,0:T(8,128)(2,1)}, u32[]{:S(2)}, u32[]{:S(2)}) collective-permute-start(bf16[256,1024]{1,0:T(8,128)(2,1)} %collective-permute-done.13.refs_0_.refs_3_), channel_id=1, source_target_pairs={{0,4},{4,0},{8,12},{12,8},{16,20},{20,16},{24,28},{28,24},{1,5},{5... | collective-permute-start | bytes 1572872 | tf_op jit(solution)/shard_map/ppermute | solution.py:246
  157.2 50.9 %collective-permute-start.16 = (bf16[128,1536]{1,0:T(8,128)(2,1)}, bf16[128,1536]{1,0:T(8,128)(2,1)}, u32[]{:S(2)}, u32[]{:S(2)}) collective-permute-start(bf16[128,1536]{1,0:T(8,128)(2,1)} %get-tuple-element.28), channel_id=1, source_target_pairs={{0,8},{4,12},{8,0},{12,4},{16,24},{20,28},{24,16},{28,20},{1,9},{5... | collective-permute-start | bytes 1179656 | tf_op jit(solution)/shard_map/ppermute | solution.py:243
  167.2 43.9 %collective-permute-start.24 = (bf16[256,1024]{1,0:T(8,128)(2,1)}, bf16[256,1024]{1,0:T(8,128)(2,1)}, u32[]{:S(2)}, u32[]{:S(2)}) collective-permute-start(bf16[256,1024]{1,0:T(8,128)(2,1)} %get-tuple-element.37), channel_id=1, source_target_pairs={{0,1},{3,2},{4,5},{7,6},{8,9},{11,10},{12,13},{15,14},{16,17},{19,... | collective-permute-start | bytes 1572872 | tf_op jit(solution)/shard_map/ppermute | solution.py:258
  192.0 22.0 %collective-permute-start.18 = (bf16[128,1536]{1,0:T(8,128)(2,1)S(1)}, bf16[128,1536]{1,0:T(8,128)(2,1)S(1)}, u32[]{:S(2)}, u32[]{:S(2)}) collective-permute-start(bf16[128,1536]{1,0:T(8,128)(2,1)S(1)} %copy-done.23), channel_id=1, source_target_pairs={{0,16},{4,20},{8,24},{12,28},{16,0},{20,4},{24,8},{28,12},{1,17},{... | collective-permute-start | bytes 1179656 | tf_op jit(solution)/shard_map/ppermute | solution.py:243
  202.1 12.7 %collective-permute-start.12 = (bf16[128,1536]{1,0:T(8,128)(2,1)S(1)}, bf16[128,1536]{1,0:T(8,128)(2,1)S(1)}, u32[]{:S(2)}, u32[]{:S(2)}) collective-permute-start(bf16[128,1536]{1,0:T(8,128)(2,1)S(1)} %get-tuple-element.25), channel_id=1, source_target_pairs={{0,8},{4,12},{8,0},{12,4},{16,24},{20,28},{24,16},{28,20},{1,9},{5... | collective-permute-start | bytes 1179656 | tf_op jit(solution)/shard_map/ppermute | solution.py:243
  202.7 26.3 %collective-permute-start.20 = (bf16[128,1536]{1,0:T(8,128)(2,1)S(1)}, bf16[128,1536]{1,0:T(8,128)(2,1)S(1)}, u32[]{:S(2)}, u32[]{:S(2)}) collective-permute-start(bf16[128,1536]{1,0:T(8,128)(2,1)S(1)} %get-tuple-element.32), channel_id=1, source_target_pairs={{0,16},{4,20},{8,24},{12,28},{16,0},{20,4},{24,8},{28,12},{1,17},{... | collective-permute-start | bytes 1179656 | tf_op jit(solution)/shard_map/ppermute | solution.py:243
  209.2 12.4 %collective-permute-start.17 = (bf16[128,1536]{1,0:T(8,128)(2,1)S(1)}, bf16[128,1536]{1,0:T(8,128)(2,1)S(1)}, u32[]{:S(2)}, u32[]{:S(2)}) collective-permute-start(bf16[128,1536]{1,0:T(8,128)(2,1)S(1)} %add_convert_fusion.7), channel_id=1, source_target_pairs={{0,16},{4,20},{8,24},{12,28},{16,0},{20,4},{24,8},{28,12},{1,17},{... | collective-permute-start | bytes 1179656 | tf_op jit(solution)/shard_map/ppermute | solution.py:243
  211.1 11.8 %collective-permute-start.27 = (bf16[256,1024]{1,0:T(8,128)(2,1)S(1)}, bf16[256,1024]{1,0:T(8,128)(2,1)S(1)}, u32[]{:S(2)}, u32[]{:S(2)}) collective-permute-start(bf16[256,1024]{1,0:T(8,128)(2,1)S(1)} %copy-done.33), channel_id=1, source_target_pairs={{0,1},{3,2},{4,5},{7,6},{8,9},{11,10},{12,13},{15,14},{16,17},{19,... | collective-permute-start | bytes 1572872 | tf_op jit(solution)/shard_map/ppermute | solution.py:258
  214.8 14.2 %collective-permute-start.19 = (bf16[128,1536]{1,0:T(8,128)(2,1)S(1)}, bf16[128,1536]{1,0:T(8,128)(2,1)S(1)}, u32[]{:S(2)}, u32[]{:S(2)}) collective-permute-start(bf16[128,1536]{1,0:T(8,128)(2,1)S(1)} %add_convert_fusion.5), channel_id=1, source_target_pairs={{0,8},{4,12},{8,0},{12,4},{16,24},{20,28},{24,16},{28,20},{1,9},{5... | collective-permute-start | bytes 1179656 | tf_op jit(solution)/shard_map/ppermute | solution.py:243
  223.6 14.9 %collective-permute-start.26 = (bf16[256,1024]{1,0:T(8,128)(2,1)S(1)}, bf16[256,1024]{1,0:T(8,128)(2,1)S(1)}, u32[]{:S(2)}, u32[]{:S(2)}) collective-permute-start(bf16[256,1024]{1,0:T(8,128)(2,1)S(1)} %get-tuple-element.35), channel_id=1, source_target_pairs={{1,0},{0,1},{3,2},{2,3},{5,4},{4,5},{7,6},{6,7},{9,8},{8,9},{11,10... | collective-permute-start | bytes 1572872 | tf_op jit(solution)/shard_map/ppermute | solution.py:258
  (45 other events, 439.1 us)

commit v2 on v1

--- a/solution.py
+++ b/solution.py
@@ -13,7 +13,8 @@
 F32 = jnp.float32
 KIND_ROWS = 8
 PROJECT_TILE = 512
-WEIGHT_TILE = 256
+CHOOSE_STEPS = 2
+WEIGHT_TILE = 512
 
 
 def pack_kernel(kinds_of_loops, dest, grads, *outs, capacity):
@@ -33,14 +34,22 @@
 def packed_grads(out_grad, dest_row, loop_modality, capacity):
     rows, columns = out_grad.shape
     slots = dest_row.reshape(1, -1)
-    vmem = pl.BlockSpec(memory_space=pltpu.VMEM)
+    packed = (rows // 2 + KIND_ROWS, columns)
     return pl.pallas_call(
         functools.partial(pack_kernel, capacity=capacity),
-        out_shape=[jax.ShapeDtypeStruct((rows // 2 + KIND_ROWS, columns), BF16)] * 2,
-        in_specs=[pl.BlockSpec(memory_space=pltpu.SMEM), vmem, vmem],
-        out_specs=[vmem, vmem],
+        grid_spec=pltpu.PrefetchScalarGridSpec(
+            num_scalar_prefetch=1,
+            grid=(1,),
+            in_specs=[whole(slots.shape), whole(out_grad.shape)],
+            out_specs=[whole(packed), whole(packed)],
+        ),
+        out_shape=[jax.ShapeDtypeStruct(packed, BF16)] * 2,
         compiler_params=limit(8),
     )(loop_modality, slots, out_grad)
+
+
+def in_hbm(value):
+    return pltpu.with_memory_space_constraint(value, pltpu.HBM)
 
 
 def kinds_in(refs):
@@ -107,7 +116,7 @@
         ),
         out_shape=[jax.ShapeDtypeStruct((size, 2 * half), BF16) for size in sizes],
         compiler_params=limit(28),
-    )(core, own_weight, other_weight, *blocks)
+    )(core, in_hbm(own_weight), in_hbm(other_weight), *blocks)
 
 
 def project_kernel(core, own_weight, other_weight, *refs, blocks, halves):
@@ -144,29 +153,30 @@
         ),
         out_shape=[jax.ShapeDtypeStruct((size, columns), BF16) for size in sizes],
         compiler_params=limit(28),
-    )(core, own_weight, other_weight, *blocks, *half_blocks)
+    )(core, in_hbm(own_weight), in_hbm(other_weight), *blocks, *half_blocks)
 
 
 def choose_kernel(wanted, *refs, sources):
-    outs, done = refs[sources:-1], refs[-1]
-    for place, out in enumerate(outs):
+    for place, out in enumerate(refs[sources:]):
         for index, source in enumerate(refs[:sources]):
             @pl.when(wanted[place] == index)
-            def _(place=place, out=out, source=source):
-                pltpu.make_async_copy(source, out, done.at[place]).start()
-    for place, out in enumerate(outs):
-        pltpu.make_async_copy(refs[0], out, done.at[place]).wait()
+            def _(out=out, source=source):
+                out[...] = source[...]
 
 
 def choose(wanted, sources, count):
-    any_space = pl.BlockSpec(memory_space=pl.ANY)
+    rows, columns = sources[0].shape
+    spec = pl.BlockSpec((rows // CHOOSE_STEPS, columns), lambda step, wanted: (step, 0))
     return pl.pallas_call(
         functools.partial(choose_kernel, sources=len(sources)),
-        in_specs=[pl.BlockSpec(memory_space=pltpu.SMEM)] + [any_space] * len(sources),
-        out_specs=[any_space] * count,
-        out_shape=[jax.ShapeDtypeStruct(sources[0].shape, sources[0].dtype)] * count,
-        scratch_shapes=[pltpu.SemaphoreType.DMA((count,))],
-        compiler_params=limit(4),
+        grid_spec=pltpu.PrefetchScalarGridSpec(
+            num_scalar_prefetch=1,
+            grid=(CHOOSE_STEPS,),
+            in_specs=[spec] * len(sources),
+            out_specs=[spec] * count,
+        ),
+        out_shape=[jax.ShapeDtypeStruct((rows, columns), sources[0].dtype)] * count,
+        compiler_params=limit(20),
     )(wanted, *sources)
 
 

time: 242 us -> 209 us (0.86)
  starting transfers between devices: 59.1 us -> 43.5 us
  Pallas kernels: 69.8 us -> 58.5 us
  local copies, waits for them, and re-layouts: 22.8 us -> 16.6 us
    ppermute x18, starting transfers between devices: 40.4 us -> 24.2 us  [across(): return lax.ppermute(value, 'loop', pairs)]
    pallas_call x2, Pallas kernels: 18.2 us -> 3.77 us  [the longest x1 3.18 us: choose(): pl.pallas_call(functools.partial(choose_kernel, sources=len(sources)), gr...]
    unnamed x72 -> x60, local copies, waits for them, and re-layouts: 22.8 us -> 16.6 us
  transfers between devices with their start and end apart: 41 -> 41, of which waited for: 15 -> 14; matrix products, arithmetic and copies ran while one was open for 2% -> 3% of each run, Pallas kernels for 29% -> 28%
where the time goes in v2:
time: 209 us; the launch traced here: 208 us
  waiting for transfers between devices  81 us (39%)
  Pallas kernels  58.5 us (28%)
  starting transfers between devices  43.5 us (21%)
  local copies, waits for them, and re-layouts  16.6 us (8%)
  other arithmetic  7.37 us (4%)
    ppermute x18, waiting for transfers between devices, across(): return lax.ppermute(value, 'loop', pairs)  51.8 us
    ppermute x10, waiting for transfers between devices, along(): return lax.ppermute(value, 'tp', pairs)  28.4 us
    ppermute x18, starting transfers between devices, across(): return lax.ppermute(value, 'loop', pairs)  24.2 us
    pallas_call x3, Pallas kernels, project_parts(): pl.pallas_call(functools.partial(project_kernel, blocks=len(blocks), halv...  20.4 us
    pallas_call x3, Pallas kernels, input_terms(): pl.pallas_call(functools.partial(input_kernel, blocks=len(blocks), tile=t...  18.8 us
    ppermute x10, starting transfers between devices, along(): return lax.ppermute(value, 'tp', pairs)  18.1 us
    unnamed x60, local copies, waits for them, and re-layouts  16.6 us
    pallas_call x1, Pallas kernels, weight_gradient(): pl.pallas_call(functools.partial(weight_kernel, blocks=len(blocks), grads...  15.4 us
  transfers between devices with their start and end apart: 41, of which 14 were waited for; matrix products, arithmetic and copies ran while one was open for 3% of the time, Pallas kernels for 28%

profile of v2, /device:TPU:0, one launch (start us, length us, event | category | flops | bytes accessed | tf_op | source)
XLA Modules:
  0.0 207.8 jit_solution(6151903846862129340)
XLA Ops:
  4.3 3.0 %collective-permute-start.10 = (bf16[136,1536]{1,0:T(8,128)(2,1)S(1)}, bf16[136,1536]{1,0:T(8,128)(2,1)S(1)}, u32[]{:S(2)}, u32[]{:S(2)}) collective-permute-start(bf16[136,1536]{1,0:T(8,128)(2,1)S(1)} %get-tuple-element.20.refs_1_.refs_0_.refs_8_.refs_24_), channel_id=1, source_target_pairs={{0,16},{4,20},{8,24},{12,28},{16,0},{20,4},{24,8},{28,12},{1,17},{... | collective-permute-start | bytes 1253384 | tf_op jit(solution)/shard_map/ppermute | solution.py:253
  7.3 1.5 collective-permute-start.8
  10.3 2.9 %collective-permute-start.1 = (bf16[256,1024]{1,0:T(8,128)(2,1)}, bf16[256,1024]{1,0:T(8,128)(2,1)S(1)}, u32[]{:S(2)}, u32[]{:S(2)}) collective-permute-start(bf16[256,1024]{1,0:T(8,128)(2,1)} %refs_0_.1), channel_id=1, source_target_pairs={{0,1},{1,0},{2,3},{3,2},{4,5},{5,4},{6,7},{7,6},{8,9},{9,8},{10,11... | collective-permute-start | bytes 1572872 | tf_op jit(solution)/shard_map/ppermute | solution.py:268
  13.2 4.0 %collective-permute-done.10.refs_4_.refs_2_.refs_12_.refs_28_ = bf16[136,1536]{1,0:T(8,128)(2,1)S(1)} collective-permute-done((bf16[136,1536]{1,0:T(8,128)(2,1)S(1)}, bf16[136,1536]{1,0:T(8,128)(2,1)S(1)}, u32[]{:S(2)}, u32[]{:S(2)}) %collective-permute-start.10) | collective-permute-done | bytes 417824 | tf_op jit(solution)/shard_map/ppermute | solution.py:253
  17.2 1.7 collective-permute-start.11
  19.0 1.5 collective-permute-start.9
  22.7 3.0 %collective-permute-done.1.refs_1_ = bf16[256,1024]{1,0:T(8,128)(2,1)S(1)} collective-permute-done((bf16[256,1024]{1,0:T(8,128)(2,1)}, bf16[256,1024]{1,0:T(8,128)(2,1)S(1)}, u32[]{:S(2)}, u32[]{:S(2)}) %collective-permute-start.1) | collective-permute-done | bytes 524320 | tf_op jit(solution)/shard_map/ppermute | solution.py:268
  34.4 6.0 %collective-permute-done.14.refs_1_.refs_0_.refs_14_.refs_30_ = bf16[136,1536]{1,0:T(8,128)(2,1)S(1)} collective-permute-done((bf16[136,1536]{1,0:T(8,128)(2,1)S(1)}, bf16[136,1536]{1,0:T(8,128)(2,1)S(1)}, u32[]{:S(2)}, u32[]{:S(2)}) %collective-permute-start.14) | collective-permute-done | bytes 417824 | tf_op jit(solution)/shard_map/ppermute | solution.py:253
  42.5 8.4 %collective-permute-done.15.refs_2_.refs_1_.refs_15_.refs_31_ = bf16[136,1536]{1,0:T(8,128)(2,1)S(1)} collective-permute-done((bf16[136,1536]{1,0:T(8,128)(2,1)S(1)}, bf16[136,1536]{1,0:T(8,128)(2,1)S(1)}, u32[]{:S(2)}, u32[]{:S(2)}) %collective-permute-start.15) | collective-permute-done | bytes 417824 | tf_op jit(solution)/shard_map/ppermute | solution.py:253
  51.0 4.0 %collective-permute-done.3.refs_3_ = bf16[256,1024]{1,0:T(8,128)(2,1)} collective-permute-done((bf16[256,1024]{1,0:T(8,128)(2,1)}, bf16[256,1024]{1,0:T(8,128)(2,1)}, u32[]{:S(2)}, u32[]{:S(2)}) %collective-permute-start.3) | collective-permute-done | bytes 524320 | tf_op jit(solution)/shard_map/ppermute | solution.py:268
  55.0 11.1 %collective-permute-done.5.refs_5_ = bf16[256,1024]{1,0:T(8,128)(2,1)} collective-permute-done((bf16[256,1024]{1,0:T(8,128)(2,1)}, bf16[256,1024]{1,0:T(8,128)(2,1)}, u32[]{:S(2)}, u32[]{:S(2)}) %collective-permute-start.5) | collective-permute-done | bytes 524320 | tf_op jit(solution)/shard_map/ppermute | solution.py:268
  68.2 3.2 %shard_map.76 = (bf16[256,1024]{1,0:T(8,128)(2,1)}, bf16[256,1024]{1,0:T(8,128)(2,1)}, bf16[256,1024]{1,0:T(8,128)(2,1)}, bf16[256,1024]{1,0:T(8,128)(2,1)S(1)}) custom-call(s32[4]{0:T(128)S(1)} %pad_add_fusion.wanted, bf16[256,1024]{1,0:T(8,128)(2,1)S(1)} %copy-done.11, bf16[256,1024]{1,0:T(8,128)(2,1)S(1)} %copy-done.13, ...), custom_call_target="tpu_custom_call" | custom-call | tf_op jit(solution)/shard_map/pallas_call | solution.py:170
  73.2 7.9 %shard_map.82 = (bf16[256,1024]{1,0:T(8,128)(2,1)S(1)}, bf16[256,1024]{1,0:T(8,128)(2,1)S(1)}) custom-call(s32[1]{0:T(128)} %bitcast.core, bf16[3,512,1536]{2,1,0:T(8,128)(2,1)} %own_weight.11, bf16[3,512,1536]{2,1,0:T(8,128)(2,1)} %collective-permute-done.other_weight, bf16[136,1536]{1,0:T(8,128)(2,1)S(1)} %collective-permute-done.8.refs_2_.refs_0_.refs_10_.refs_26_, ...), custom_call_target="tpu_custom_call" | custom-call | tf_op jit(solution)/shard_map/pallas_call | solution.py:109
  81.1 2.6 %collective-permute-start.13 = (bf16[256,1024]{1,0:T(8,128)(2,1)S(1)}, bf16[256,1024]{1,0:T(8,128)(2,1)}, u32[]{:S(2)}, u32[]{:S(2)}) collective-permute-start(bf16[256,1024]{1,0:T(8,128)(2,1)S(1)} %copy-done.17), channel_id=1, source_target_pairs={{0,24},{4,28},{8,16},{12,20},{16,8},{20,12},{24,0},{28,4},{1,25},{... | collective-permute-start | bytes 1572872 | tf_op jit(solution)/shard_map/ppermute | solution.py:253
  84.7 5.4 %shard_map.81 = bf16[256,1024]{1,0:T(8,128)(2,1)S(1)} custom-call(s32[1]{0:T(128)} %bitcast.core, bf16[3,512,1536]{2,1,0:T(8,128)(2,1)} %own_weight.11, bf16[3,512,1536]{2,1,0:T(8,128)(2,1)} %collective-permute-done.other_weight, bf16[136,1536]{1,0:T(8,128)(2,1)S(1)} %collective-permute-done.14.refs_1_.refs_0_.refs_14_.refs_30_, ...), custom_call_target="tpu_custom_call" | custom-call | tf_op jit(solution)/shard_map/pallas_call | solution.py:109
  90.1 2.5 %collective-permute-start.21 = (bf16[256,1024]{1,0:T(8,128)(2,1)S(1)}, bf16[256,1024]{1,0:T(8,128)(2,1)S(1)}, u32[]{:S(2)}, u32[]{:S(2)}) collective-permute-start(bf16[256,1024]{1,0:T(8,128)(2,1)S(1)} %shard_map.81), channel_id=1, source_target_pairs={{0,24},{4,28},{8,16},{12,20},{16,8},{20,12},{24,0},{28,4},{1,25},{... | collective-permute-start | bytes 1572872 | tf_op jit(solution)/shard_map/ppermute | solution.py:253
  92.6 6.4 %collective-permute-done.7.refs_1_.refs_2_ = bf16[256,1024]{1,0:T(8,128)(2,1)} collective-permute-done((bf16[256,1024]{1,0:T(8,128)(2,1)}, bf16[256,1024]{1,0:T(8,128)(2,1)}, u32[]{:S(2)}, u32[]{:S(2)}) %collective-permute-start.7) | collective-permute-done | bytes 524320 | tf_op jit(solution)/shard_map/ppermute | solution.py:253
  99.6 21.1 %collective-permute-done.22 = bf16[256,1024]{1,0:T(8,128)(2,1)S(1)} collective-permute-done((bf16[256,1024]{1,0:T(8,128)(2,1)S(1)}, bf16[256,1024]{1,0:T(8,128)(2,1)S(1)}, u32[]{:S(2)}, u32[]{:S(2)}) %collective-permute-start.22) | collective-permute-done | bytes 524320 | tf_op jit(solution)/shard_map/ppermute | solution.py:253
  121.5 6.7 %shard_map.80 = (bf16[128,1536]{1,0:T(8,128)(2,1)}, bf16[128,1536]{1,0:T(8,128)(2,1)S(1)}) custom-call(s32[1]{0:T(128)} %bitcast.core, bf16[3,512,1536]{2,1,0:T(8,128)(2,1)} %own_weight.11, bf16[3,512,1536]{2,1,0:T(8,128)(2,1)} %collective-permute-done.other_weight, bf16[256,1024]{1,0:T(8,128)(2,1)} %collective-permute-done.13.refs_0_.refs_3_, ...), custom_call_target="tpu_custom_call" | custom-call | tf_op jit(solution)/shard_map/pallas_call | solution.py:144
  129.8 1.5 collective-permute-start.16
  131.3 5.5 %shard_map.83 = bf16[256,1024]{1,0:T(8,128)(2,1)S(1)} custom-call(s32[1]{0:T(128)} %bitcast.core, bf16[3,512,1536]{2,1,0:T(8,128)(2,1)} %own_weight.11, bf16[3,512,1536]{2,1,0:T(8,128)(2,1)} %collective-permute-done.other_weight, bf16[136,1536]{1,0:T(8,128)(2,1)S(1)} %get-tuple-element.20.refs_1_.refs_0_.refs_8_.refs_24_, ...), custom_call_target="tpu_custom_call" | custom-call | tf_op jit(solution)/shard_map/pallas_call | solution.py:109
  138.1 2.3 %collective-permute-start.24 = (bf16[256,1024]{1,0:T(8,128)(2,1)}, bf16[256,1024]{1,0:T(8,128)(2,1)}, u32[]{:S(2)}, u32[]{:S(2)}) collective-permute-start(bf16[256,1024]{1,0:T(8,128)(2,1)} %get-tuple-element.37), channel_id=1, source_target_pairs={{0,1},{3,2},{4,5},{7,6},{8,9},{11,10},{12,13},{15,14},{16,17},{19,... | collective-permute-start | bytes 1572872 | tf_op jit(solution)/shard_map/ppermute | solution.py:268
  145.4 15.4 %shard_map.84 = bf16[3,512,1536]{2,1,0:T(8,128)(2,1)} custom-call(s32[1]{0:T(128)} %bitcast.core, bf16[256,1024]{1,0:T(8,128)(2,1)} %get-tuple-element.19.refs_0_, bf16[256,1024]{1,0:T(8,128)(2,1)} %collective-permute-done.6.refs_0_.refs_1_, bf16[256,1024]{1,0:T(8,128)(2,1)} %collective-permute-done.7.refs_1_.refs_2_, ...), custom_call_target="tpu_custom_call" | custom-call | tf_op jit(solution)/shard_map/pallas_call | solution.py:214
  161.4 7.8 %shard_map.79 = (bf16[128,1536]{1,0:T(8,128)(2,1)S(1)}, bf16[128,1536]{1,0:T(8,128)(2,1)S(1)}, bf16[128,1536]{1,0:T(8,128)(2,1)S(1)}, bf16[128,1536]{1,0:T(8,128)(2,1)S(1)}) custom-call(s32[1]{0:T(128)} %bitcast.core, bf16[3,512,1536]{2,1,0:T(8,128)(2,1)} %own_weight.11, bf16[3,512,1536]{2,1,0:T(8,128)(2,1)} %collective-permute-done.other_weight, ...), custom_call_target="tpu_custom_call" | custom-call | tf_op jit(solution)/shard_map/pallas_call | solution.py:144
  169.3 2.1 collective-permute-start.20
  171.4 5.9 %shard_map.78 = (bf16[128,1536]{1,0:T(8,128)(2,1)S(1)}, bf16[128,1536]{1,0:T(8,128)(2,1)S(1)}) custom-call(s32[1]{0:T(128)} %bitcast.core, bf16[3,512,1536]{2,1,0:T(8,128)(2,1)} %own_weight.11, bf16[3,512,1536]{2,1,0:T(8,128)(2,1)} %collective-permute-done.other_weight, bf16[256,1024]{1,0:T(8,128)(2,1)} %get-tuple-element.19.refs_0_, ...), custom_call_target="tpu_custom_call" | custom-call | tf_op jit(solution)/shard_map/pallas_call | solution.py:144
  180.0 1.5 add_convert_fusion.3
  182.4 2.0 collective-permute-start.19
  184.3 4.3 %collective-permute-done.17 = bf16[128,1536]{1,0:T(8,128)(2,1)S(1)} collective-permute-done((bf16[128,1536]{1,0:T(8,128)(2,1)S(1)}, bf16[128,1536]{1,0:T(8,128)(2,1)S(1)}, u32[]{:S(2)}, u32[]{:S(2)}) %collective-permute-start.17) | collective-permute-done | bytes 393248 | tf_op jit(solution)/shard_map/ppermute | solution.py:253
  188.8 1.8 collective-permute-done.27
  191.3 4.7 %collective-permute-start.26 = (bf16[256,1024]{1,0:T(8,128)(2,1)S(1)}, bf16[256,1024]{1,0:T(8,128)(2,1)S(1)}, u32[]{:S(2)}, u32[]{:S(2)}) collective-permute-start(bf16[256,1024]{1,0:T(8,128)(2,1)S(1)} %get-tuple-element.35), channel_id=1, source_target_pairs={{1,0},{0,1},{3,2},{2,3},{5,4},{4,5},{7,6},{6,7},{9,8},{8,9},{11,10... | collective-permute-start | bytes 1572872 | tf_op jit(solution)/shard_map/ppermute | solution.py:268
  197.8 8.6 %collective-permute-done.26 = bf16[256,1024]{1,0:T(8,128)(2,1)S(1)} collective-permute-done((bf16[256,1024]{1,0:T(8,128)(2,1)S(1)}, bf16[256,1024]{1,0:T(8,128)(2,1)S(1)}, u32[]{:S(2)}, u32[]{:S(2)}) %collective-permute-start.26) | collective-permute-done | bytes 524320 | tf_op jit(solution)/shard_map/ppermute | solution.py:268
  (129 shorter events, 40.6 us)
Async XLA Ops:
  0.6 72.1 %collective-permute-start = (bf16[3,512,1536]{2,1,0:T(8,128)(2,1)}, bf16[3,512,1536]{2,1,0:T(8,128)(2,1)}, u32[]{:S(2)}, u32[]{:S(2)}) collective-permute-start(bf16[3,512,1536]{2,1,0:T(8,128)(2,1)} %own_weight.11), channel_id=1, source_target_pairs={{0,4},{4,0},{8,12},{12,8},{16,20},{20,16},{24,28},{28,24},{1,5},{5... | collective-permute-start | bytes 14155784 | tf_op jit(solution)/shard_map/ppermute | solution.py:256
  4.3 12.9 %collective-permute-start.10 = (bf16[136,1536]{1,0:T(8,128)(2,1)S(1)}, bf16[136,1536]{1,0:T(8,128)(2,1)S(1)}, u32[]{:S(2)}, u32[]{:S(2)}) collective-permute-start(bf16[136,1536]{1,0:T(8,128)(2,1)S(1)} %get-tuple-element.20.refs_1_.refs_0_.refs_8_.refs_24_), channel_id=1, source_target_pairs={{0,16},{4,20},{8,24},{12,28},{16,0},{20,4},{24,8},{28,12},{1,17},{... | collective-permute-start | bytes 1253384 | tf_op jit(solution)/shard_map/ppermute | solution.py:253
  7.3 11.6 %collective-permute-start.8 = (bf16[136,1536]{1,0:T(8,128)(2,1)S(1)}, bf16[136,1536]{1,0:T(8,128)(2,1)S(1)}, u32[]{:S(2)}, u32[]{:S(2)}) collective-permute-start(bf16[136,1536]{1,0:T(8,128)(2,1)S(1)} %get-tuple-element.20.refs_1_.refs_0_.refs_8_.refs_24_), channel_id=1, source_target_pairs={{0,8},{4,12},{8,0},{12,4},{16,24},{20,28},{24,16},{28,20},{1,9},{5... | collective-permute-start | bytes 1253384 | tf_op jit(solution)/shard_map/ppermute | solution.py:253
  8.8 11.6 %collective-permute-start.34 = (bf16[136,1536]{1,0:T(8,128)(2,1)S(1)}, bf16[136,1536]{1,0:T(8,128)(2,1)S(1)}, u32[]{:S(2)}, u32[]{:S(2)}) collective-permute-start(bf16[136,1536]{1,0:T(8,128)(2,1)S(1)} %get-tuple-element.21.refs_2_.refs_1_.refs_9_.refs_25_), channel_id=1, source_target_pairs={{0,4},{4,0},{8,12},{12,8},{16,20},{20,16},{24,28},{28,24},{1,5},{5... | collective-permute-start | bytes 1253384 | tf_op jit(solution)/shard_map/ppermute | solution.py:256
  10.3 15.4 %collective-permute-start.1 = (bf16[256,1024]{1,0:T(8,128)(2,1)}, bf16[256,1024]{1,0:T(8,128)(2,1)S(1)}, u32[]{:S(2)}, u32[]{:S(2)}) collective-permute-start(bf16[256,1024]{1,0:T(8,128)(2,1)} %refs_0_.1), channel_id=1, source_target_pairs={{0,1},{1,0},{2,3},{3,2},{4,5},{5,4},{6,7},{7,6},{8,9},{9,8},{10,11... | collective-permute-start | bytes 1572872 | tf_op jit(solution)/shard_map/ppermute | solution.py:268
  17.2 11.1 %collective-permute-start.11 = (bf16[136,1536]{1,0:T(8,128)(2,1)S(1)}, bf16[136,1536]{1,0:T(8,128)(2,1)S(1)}, u32[]{:S(2)}, u32[]{:S(2)}) collective-permute-start(bf16[136,1536]{1,0:T(8,128)(2,1)S(1)} %get-tuple-element.21.refs_2_.refs_1_.refs_9_.refs_25_), channel_id=1, source_target_pairs={{0,16},{4,20},{8,24},{12,28},{16,0},{20,4},{24,8},{28,12},{1,17},{... | collective-permute-start | bytes 1253384 | tf_op jit(solution)/shard_map/ppermute | solution.py:253
  29.5 10.9 %collective-permute-start.14 = (bf16[136,1536]{1,0:T(8,128)(2,1)S(1)}, bf16[136,1536]{1,0:T(8,128)(2,1)S(1)}, u32[]{:S(2)}, u32[]{:S(2)}) collective-permute-start(bf16[136,1536]{1,0:T(8,128)(2,1)S(1)} %collective-permute-done.10.refs_4_.refs_2_.refs_12_.refs_28_), channel_id=1, source_target_pairs={{0,8},{4,12},{8,0},{12,4},{16,24},{20,28},{24,16},{28,20},{1,9},{5... | collective-permute-start | bytes 1253384 | tf_op jit(solution)/shard_map/ppermute | solution.py:253
  31.0 10.8 %collective-permute-start.35 = (bf16[136,1536]{1,0:T(8,128)(2,1)S(1)}, bf16[136,1536]{1,0:T(8,128)(2,1)S(1)}, u32[]{:S(2)}, u32[]{:S(2)}) collective-permute-start(bf16[136,1536]{1,0:T(8,128)(2,1)S(1)} %collective-permute-done.8.refs_2_.refs_0_.refs_10_.refs_26_), channel_id=1, source_target_pairs={{0,4},{4,0},{8,12},{12,8},{16,20},{20,16},{24,28},{28,24},{1,5},{5... | collective-permute-start | bytes 1253384 | tf_op jit(solution)/shard_map/ppermute | solution.py:256
  31.8 23.2 %collective-permute-start.3 = (bf16[256,1024]{1,0:T(8,128)(2,1)}, bf16[256,1024]{1,0:T(8,128)(2,1)}, u32[]{:S(2)}, u32[]{:S(2)}) collective-permute-start(bf16[256,1024]{1,0:T(8,128)(2,1)} %collective-permute-done.2.refs_2_), channel_id=1, source_target_pairs={{1,0},{2,3},{5,4},{6,7},{9,8},{10,11},{13,12},{14,15},{17,16},{18,... | collective-permute-start | bytes 1572872 | tf_op jit(solution)/shard_map/ppermute | solution.py:268
  33.1 33.0 %collective-permute-start.5 = (bf16[256,1024]{1,0:T(8,128)(2,1)}, bf16[256,1024]{1,0:T(8,128)(2,1)}, u32[]{:S(2)}, u32[]{:S(2)}) collective-permute-start(bf16[256,1024]{1,0:T(8,128)(2,1)} %collective-permute-done.4.refs_4_), channel_id=1, source_target_pairs={{1,0},{2,3},{5,4},{6,7},{9,8},{10,11},{13,12},{14,15},{17,16},{18,... | collective-permute-start | bytes 1572872 | tf_op jit(solution)/shard_map/ppermute | solution.py:268
  42.5 29.6 %collective-permute-start.38 = (bf16[136,1536]{1,0:T(8,128)(2,1)S(1)}, bf16[136,1536]{1,0:T(8,128)(2,1)}, u32[]{:S(2)}, u32[]{:S(2)}) collective-permute-start(bf16[136,1536]{1,0:T(8,128)(2,1)S(1)} %collective-permute-done.11.refs_5_.refs_3_.refs_13_.refs_29_), channel_id=1, source_target_pairs={{0,4},{4,0},{8,12},{12,8},{16,20},{20,16},{24,28},{28,24},{1,5},{5... | collective-permute-start | bytes 1253384 | tf_op jit(solution)/shard_map/ppermute | solution.py:256
  51.0 30.1 %collective-permute-start.36 = (bf16[136,1536]{1,0:T(8,128)(2,1)S(1)}, bf16[136,1536]{1,0:T(8,128)(2,1)}, u32[]{:S(2)}, u32[]{:S(2)}) collective-permute-start(bf16[136,1536]{1,0:T(8,128)(2,1)S(1)} %collective-permute-done.9.refs_3_.refs_1_.refs_11_.refs_27_), channel_id=1, source_target_pairs={{0,4},{4,0},{8,12},{12,8},{16,20},{20,16},{24,28},{28,24},{1,5},{5... | collective-permute-start | bytes 1253384 | tf_op jit(solution)/shard_map/ppermute | solution.py:256
  55.0 28.7 %collective-permute-start.39 = (bf16[136,1536]{1,0:T(8,128)(2,1)S(1)}, bf16[136,1536]{1,0:T(8,128)(2,1)}, u32[]{:S(2)}, u32[]{:S(2)}) collective-permute-start(bf16[136,1536]{1,0:T(8,128)(2,1)S(1)} %collective-permute-done.14.refs_1_.refs_0_.refs_14_.refs_30_), channel_id=1, source_target_pairs={{0,4},{4,0},{8,12},{12,8},{16,20},{20,16},{24,28},{28,24},{1,5},{5... | collective-permute-start | bytes 1253384 | tf_op jit(solution)/shard_map/ppermute | solution.py:256
  66.0 18.1 %collective-permute-start.40 = (bf16[136,1536]{1,0:T(8,128)(2,1)S(1)}, bf16[136,1536]{1,0:T(8,128)(2,1)}, u32[]{:S(2)}, u32[]{:S(2)}) collective-permute-start(bf16[136,1536]{1,0:T(8,128)(2,1)S(1)} %collective-permute-done.15.refs_2_.refs_1_.refs_15_.refs_31_), channel_id=1, source_target_pairs={{0,4},{4,0},{8,12},{12,8},{16,20},{20,16},{24,28},{28,24},{1,5},{5... | collective-permute-start | bytes 1253384 | tf_op jit(solution)/shard_map/ppermute | solution.py:256
  72.2 17.9 %collective-permute-start.6 = (bf16[256,1024]{1,0:T(8,128)(2,1)}, bf16[256,1024]{1,0:T(8,128)(2,1)}, u32[]{:S(2)}, u32[]{:S(2)}) collective-permute-start(bf16[256,1024]{1,0:T(8,128)(2,1)} %get-tuple-element.23), channel_id=1, source_target_pairs={{0,8},{4,12},{8,0},{12,4},{16,24},{20,28},{24,16},{28,20},{1,9},{5... | collective-permute-start | bytes 1572872 | tf_op jit(solution)/shard_map/ppermute | solution.py:253
  72.7 26.3 %collective-permute-start.7 = (bf16[256,1024]{1,0:T(8,128)(2,1)}, bf16[256,1024]{1,0:T(8,128)(2,1)}, u32[]{:S(2)}, u32[]{:S(2)}) collective-permute-start(bf16[256,1024]{1,0:T(8,128)(2,1)} %get-tuple-element.24), channel_id=1, source_target_pairs={{0,16},{4,20},{8,24},{12,28},{16,0},{20,4},{24,8},{28,12},{1,17},{... | collective-permute-start | bytes 1572872 | tf_op jit(solution)/shard_map/ppermute | solution.py:253
  81.1 18.0 %collective-permute-start.13 = (bf16[256,1024]{1,0:T(8,128)(2,1)S(1)}, bf16[256,1024]{1,0:T(8,128)(2,1)}, u32[]{:S(2)}, u32[]{:S(2)}) collective-permute-start(bf16[256,1024]{1,0:T(8,128)(2,1)S(1)} %copy-done.17), channel_id=1, source_target_pairs={{0,24},{4,28},{8,16},{12,20},{16,8},{20,12},{24,0},{28,4},{1,25},{... | collective-permute-start | bytes 1572872 | tf_op jit(solution)/shard_map/ppermute | solution.py:253
  83.7 37.0 %collective-permute-start.22 = (bf16[256,1024]{1,0:T(8,128)(2,1)S(1)}, bf16[256,1024]{1,0:T(8,128)(2,1)S(1)}, u32[]{:S(2)}, u32[]{:S(2)}) collective-permute-start(bf16[256,1024]{1,0:T(8,128)(2,1)S(1)} %get-tuple-element.33), channel_id=1, source_target_pairs={{0,16},{4,20},{8,24},{12,28},{16,0},{20,4},{24,8},{28,12},{1,17},{... | collective-permute-start | bytes 1572872 | tf_op jit(solution)/shard_map/ppermute | solution.py:253
  84.2 36.5 %collective-permute-start.23 = (bf16[256,1024]{1,0:T(8,128)(2,1)S(1)}, bf16[256,1024]{1,0:T(8,128)(2,1)S(1)}, u32[]{:S(2)}, u32[]{:S(2)}) collective-permute-start(bf16[256,1024]{1,0:T(8,128)(2,1)S(1)} %get-tuple-element.34), channel_id=1, source_target_pairs={{0,8},{4,12},{8,0},{12,4},{16,24},{20,28},{24,16},{28,20},{1,9},{5... | collective-permute-start | bytes 1572872 | tf_op jit(solution)/shard_map/ppermute | solution.py:253
  90.1 38.9 %collective-permute-start.21 = (bf16[256,1024]{1,0:T(8,128)(2,1)S(1)}, bf16[256,1024]{1,0:T(8,128)(2,1)S(1)}, u32[]{:S(2)}, u32[]{:S(2)}) collective-permute-start(bf16[256,1024]{1,0:T(8,128)(2,1)S(1)} %shard_map.81), channel_id=1, source_target_pairs={{0,24},{4,28},{8,16},{12,20},{16,8},{20,12},{24,0},{28,4},{1,25},{... | collective-permute-start | bytes 1572872 | tf_op jit(solution)/shard_map/ppermute | solution.py:253
  99.1 39.1 %collective-permute-start.29 = (bf16[256,1024]{1,0:T(8,128)(2,1)}, bf16[256,1024]{1,0:T(8,128)(2,1)}, u32[]{:S(2)}, u32[]{:S(2)}) collective-permute-start(bf16[256,1024]{1,0:T(8,128)(2,1)} %get-tuple-element.19.refs_0_), channel_id=1, source_target_pairs={{0,4},{4,0},{8,12},{12,8},{16,20},{20,16},{24,28},{28,24},{1,5},{5... | collective-permute-start | bytes 1572872 | tf_op jit(solution)/shard_map/ppermute | solution.py:256
  99.1 41.3 %collective-permute-start.30 = (bf16[256,1024]{1,0:T(8,128)(2,1)}, bf16[256,1024]{1,0:T(8,128)(2,1)}, u32[]{:S(2)}, u32[]{:S(2)}) collective-permute-start(bf16[256,1024]{1,0:T(8,128)(2,1)} %collective-permute-done.6.refs_0_.refs_1_), channel_id=1, source_target_pairs={{0,4},{4,0},{8,12},{12,8},{16,20},{20,16},{24,28},{28,24},{1,5},{5... | collective-permute-start | bytes 1572872 | tf_op jit(solution)/shard_map/ppermute | solution.py:256
  120.7 19.7 %collective-permute-start.31 = (bf16[256,1024]{1,0:T(8,128)(2,1)}, bf16[256,1024]{1,0:T(8,128)(2,1)}, u32[]{:S(2)}, u32[]{:S(2)}) collective-permute-start(bf16[256,1024]{1,0:T(8,128)(2,1)} %collective-permute-done.7.refs_1_.refs_2_), channel_id=1, source_target_pairs={{0,4},{4,0},{8,12},{12,8},{16,20},{20,16},{24,28},{28,24},{1,5},{5... | collective-permute-start | bytes 1572872 | tf_op jit(solution)/shard_map/ppermute | solution.py:256
  121.5 18.9 %collective-permute-start.32 = (bf16[256,1024]{1,0:T(8,128)(2,1)}, bf16[256,1024]{1,0:T(8,128)(2,1)}, u32[]{:S(2)}, u32[]{:S(2)}) collective-permute-start(bf16[256,1024]{1,0:T(8,128)(2,1)} %collective-permute-done.13.refs_0_.refs_3_), channel_id=1, source_target_pairs={{0,4},{4,0},{8,12},{12,8},{16,20},{20,16},{24,28},{28,24},{1,5},{5... | collective-permute-start | bytes 1572872 | tf_op jit(solution)/shard_map/ppermute | solution.py:256
  129.8 47.6 %collective-permute-start.16 = (bf16[128,1536]{1,0:T(8,128)(2,1)}, bf16[128,1536]{1,0:T(8,128)(2,1)}, u32[]{:S(2)}, u32[]{:S(2)}) collective-permute-start(bf16[128,1536]{1,0:T(8,128)(2,1)} %get-tuple-element.28), channel_id=1, source_target_pairs={{0,8},{4,12},{8,0},{12,4},{16,24},{20,28},{24,16},{28,20},{1,9},{5... | collective-permute-start | bytes 1179656 | tf_op jit(solution)/shard_map/ppermute | solution.py:253
  138.1 40.5 %collective-permute-start.24 = (bf16[256,1024]{1,0:T(8,128)(2,1)}, bf16[256,1024]{1,0:T(8,128)(2,1)}, u32[]{:S(2)}, u32[]{:S(2)}) collective-permute-start(bf16[256,1024]{1,0:T(8,128)(2,1)} %get-tuple-element.37), channel_id=1, source_target_pairs={{0,1},{3,2},{4,5},{7,6},{8,9},{11,10},{12,13},{15,14},{16,17},{19,... | collective-permute-start | bytes 1572872 | tf_op jit(solution)/shard_map/ppermute | solution.py:268
  160.9 20.7 %collective-permute-start.18 = (bf16[128,1536]{1,0:T(8,128)(2,1)S(1)}, bf16[128,1536]{1,0:T(8,128)(2,1)S(1)}, u32[]{:S(2)}, u32[]{:S(2)}) collective-permute-start(bf16[128,1536]{1,0:T(8,128)(2,1)S(1)} %copy-done.19), channel_id=1, source_target_pairs={{0,16},{4,20},{8,24},{12,28},{16,0},{20,4},{24,8},{28,12},{1,17},{... | collective-permute-start | bytes 1179656 | tf_op jit(solution)/shard_map/ppermute | solution.py:253
  169.2 13.2 %collective-permute-start.12 = (bf16[128,1536]{1,0:T(8,128)(2,1)S(1)}, bf16[128,1536]{1,0:T(8,128)(2,1)S(1)}, u32[]{:S(2)}, u32[]{:S(2)}) collective-permute-start(bf16[128,1536]{1,0:T(8,128)(2,1)S(1)} %get-tuple-element.25), channel_id=1, source_target_pairs={{0,8},{4,12},{8,0},{12,4},{16,24},{20,28},{24,16},{28,20},{1,9},{5... | collective-permute-start | bytes 1179656 | tf_op jit(solution)/shard_map/ppermute | solution.py:253
  169.3 27.4 %collective-permute-start.20 = (bf16[128,1536]{1,0:T(8,128)(2,1)S(1)}, bf16[128,1536]{1,0:T(8,128)(2,1)S(1)}, u32[]{:S(2)}, u32[]{:S(2)}) collective-permute-start(bf16[128,1536]{1,0:T(8,128)(2,1)S(1)} %get-tuple-element.32), channel_id=1, source_target_pairs={{0,16},{4,20},{8,24},{12,28},{16,0},{20,4},{24,8},{28,12},{1,17},{... | collective-permute-start | bytes 1179656 | tf_op jit(solution)/shard_map/ppermute | solution.py:253
  178.7 11.9 %collective-permute-start.27 = (bf16[256,1024]{1,0:T(8,128)(2,1)S(1)}, bf16[256,1024]{1,0:T(8,128)(2,1)S(1)}, u32[]{:S(2)}, u32[]{:S(2)}) collective-permute-start(bf16[256,1024]{1,0:T(8,128)(2,1)S(1)} %copy-done.29), channel_id=1, source_target_pairs={{0,1},{3,2},{4,5},{7,6},{8,9},{11,10},{12,13},{15,14},{16,17},{19,... | collective-permute-start | bytes 1572872 | tf_op jit(solution)/shard_map/ppermute | solution.py:268
  182.4 14.4 %collective-permute-start.19 = (bf16[128,1536]{1,0:T(8,128)(2,1)S(1)}, bf16[128,1536]{1,0:T(8,128)(2,1)S(1)}, u32[]{:S(2)}, u32[]{:S(2)}) collective-permute-start(bf16[128,1536]{1,0:T(8,128)(2,1)S(1)} %add_convert_fusion.5), channel_id=1, source_target_pairs={{0,8},{4,12},{8,0},{12,4},{16,24},{20,28},{24,16},{28,20},{1,9},{5... | collective-permute-start | bytes 1179656 | tf_op jit(solution)/shard_map/ppermute | solution.py:253
  191.3 15.1 %collective-permute-start.26 = (bf16[256,1024]{1,0:T(8,128)(2,1)S(1)}, bf16[256,1024]{1,0:T(8,128)(2,1)S(1)}, u32[]{:S(2)}, u32[]{:S(2)}) collective-permute-start(bf16[256,1024]{1,0:T(8,128)(2,1)S(1)} %get-tuple-element.35), channel_id=1, source_target_pairs={{1,0},{0,1},{3,2},{2,3},{5,4},{4,5},{7,6},{6,7},{9,8},{8,9},{11,10... | collective-permute-start | bytes 1572872 | tf_op jit(solution)/shard_map/ppermute | solution.py:268
  (39 other events, 251.1 us)

commit v3 on v2

--- a/solution.py
+++ b/solution.py
@@ -45,11 +45,11 @@
         ),
         out_shape=[jax.ShapeDtypeStruct(packed, BF16)] * 2,
         compiler_params=limit(8),
-    )(loop_modality, slots, out_grad)
-
-
-def in_hbm(value):
-    return pltpu.with_memory_space_constraint(value, pltpu.HBM)
+    )(loop_modality, *in_hbm(slots, out_grad))
+
+
+def in_hbm(*values):
+    return [pltpu.with_memory_space_constraint(value, pltpu.HBM) for value in values]
 
 
 def kinds_in(refs):
@@ -116,44 +116,77 @@
         ),
         out_shape=[jax.ShapeDtypeStruct((size, 2 * half), BF16) for size in sizes],
         compiler_params=limit(28),
-    )(core, in_hbm(own_weight), in_hbm(other_weight), *blocks)
-
-
-def project_kernel(core, own_weight, other_weight, *refs, blocks, halves):
+    )(core, *in_hbm(own_weight, other_weight, *blocks))
+
+
+def project_kernel(core, own_weight, other_weight, *refs, counts):
     _, half, tile = own_weight.shape
+    items = len(counts)
     own_at = pl.multiple_of(core[0] * half, half)
     other_at = pl.multiple_of((1 - core[0]) * half, half)
-    own = jnp.concatenate([ref[:, pl.ds(own_at, half)] for ref in refs[:blocks]], axis=0)
-    other = jnp.concatenate([ref[:, pl.ds(other_at, half)] for ref in refs[:blocks]], axis=0)
-    kind = kinds_in([ref[...] for ref in refs[blocks:blocks + halves]])
+    own = jnp.concatenate([ref[:, pl.ds(own_at, half)] for ref in refs[:items]], axis=0)
+    other = jnp.concatenate([ref[:, pl.ds(other_at, half)] for ref in refs[:items]], axis=0)
+    kind = kinds_in([ref[...] for ref in refs[items:2 * items]])
     row_kind = jnp.broadcast_to(kind, (tile, kind.shape[1])).T
     products = [
         jnp.dot(own, own_weight[index], preferred_element_type=F32)
         + jnp.dot(other, other_weight[index], preferred_element_type=F32)
         for index in range(own_weight.shape[0])
     ]
-    chosen = pick(row_kind, products).astype(BF16)
-    for out, part in split_rows(chosen, refs[blocks + halves:]):
-        out[...] = part
-
-
-def project_parts(core, blocks, half_blocks, sizes, own_weight, other_weight):
+    pieces = iter(refs[2 * items:2 * items + sum(counts)])
+    outs = refs[2 * items + sum(counts):]
+    for count, (out, part) in zip(counts, split_rows(pick(row_kind, products), outs)):
+        for _ in range(count):
+            part = part + next(pieces)[...].astype(F32)
+        out[...] = part.astype(BF16)
+
+
+def project_parts(core, items, own_weight, other_weight):
     kinds, half, columns = own_weight.shape
     tile = math.gcd(columns, PROJECT_TILE)
     weight_spec = pl.BlockSpec((kinds, half, tile), lambda step, core: (0, 0, step))
-    return pl.pallas_call(
-        functools.partial(project_kernel, blocks=len(blocks), halves=len(half_blocks)),
+    cut = items[0][2].shape[0] - KIND_ROWS
+    column_spec = pl.BlockSpec((cut, tile), lambda step, core: (0, step))
+    row_specs = [pl.BlockSpec((cut, 2 * half), lambda step, core, part=part: (part, 0)) for _, part, _, _ in items]
+    pieces = [piece for item in items for piece in item[3]]
+    return pl.pallas_call(
+        functools.partial(project_kernel, counts=[len(item[3]) for item in items]),
         grid_spec=pltpu.PrefetchScalarGridSpec(
             num_scalar_prefetch=1,
             grid=(columns // tile,),
             in_specs=[weight_spec, weight_spec]
-            + [whole(block.shape) for block in blocks]
-            + [kind_spec(block) for block in half_blocks],
-            out_specs=[pl.BlockSpec((size, tile), lambda step, core: (0, step)) for size in sizes],
+            + row_specs
+            + [kind_spec(item[2]) for item in items]
+            + [column_spec] * len(pieces),
+            out_specs=[column_spec] * len(items),
         ),
-        out_shape=[jax.ShapeDtypeStruct((size, columns), BF16) for size in sizes],
+        out_shape=[jax.ShapeDtypeStruct((cut, columns), BF16)] * len(items),
         compiler_params=limit(28),
-    )(core, in_hbm(own_weight), in_hbm(other_weight), *blocks, *half_blocks)
+    )(core, *in_hbm(own_weight, other_weight, *[item[0] for item in items], *[item[2] for item in items], *pieces))
+
+
+def finish_kernel(*refs, count):
+    out = refs[-1]
+    cut = out.shape[0] // 2
+    for part in (0, 1):
+        total = refs[part * count][...].astype(F32)
+        for ref in refs[part * count + 1:(part + 1) * count]:
+            total = total + ref[...].astype(F32)
+        out[part * cut:(part + 1) * cut] = total.astype(BF16)
+
+
+def finish(first, second):
+    cut, columns = first[0].shape
+    tile = math.gcd(columns, PROJECT_TILE)
+    column_spec = pl.BlockSpec((cut, tile), lambda step: (0, step))
+    return pl.pallas_call(
+        functools.partial(finish_kernel, count=len(first)),
+        grid=(columns // tile,),
+        in_specs=[column_spec] * (2 * len(first)),
+        out_specs=pl.BlockSpec((2 * cut, tile), lambda step: (0, step)),
+        out_shape=jax.ShapeDtypeStruct((2 * cut, columns), BF16),
+        compiler_params=limit(12),
+    )(*in_hbm(*first, *second))
 
 
 def choose_kernel(wanted, *refs, sources):
@@ -177,7 +210,7 @@
         ),
         out_shape=[jax.ShapeDtypeStruct((rows, columns), sources[0].dtype)] * count,
         compiler_params=limit(20),
-    )(wanted, *sources)
+    )(wanted, *in_hbm(*sources))
 
 
 def weight_kernel(core, *refs, blocks, grads, scale):
@@ -224,7 +257,7 @@
         ),
         out_shape=jax.ShapeDtypeStruct((kinds, half, columns), BF16),
         compiler_params=limit(36),
-    )(core, *blocks, *half_blocks, *half_blocks)
+    )(core, *in_hbm(*blocks, *half_blocks, *half_blocks))
 
 
 def low_high(offset):
@@ -246,7 +279,6 @@
     bits = [1 << place for place in range(chip_count.bit_length() - 1)]
     offsets = sorted(range(1, chip_count), key=lambda offset: (bin(offset).count("1"), offset))
     several = [offset for offset in offsets if offset & (offset - 1)]
-    cut = row_count // 2
 
     def across(value, offset):
         pairs = [(i, i ^ (2 * offset)) for i in range(loop_count)]
@@ -295,9 +327,7 @@
 
     arrived = {}
     for group in ([0], bits, several):
-        made = input_terms(
-            core, halves_of(group), [row_count] * len(group), qkv_weight, other_weight
-        )
+        made = input_terms(core, halves_of(group), [row_count] * len(group), qkv_weight, other_weight)
         for offset, term in zip(group, made):
             arrived[offset] = across(term, offset) if offset else term
     all_terms = [arrived[offset] for offset in range(chip_count)]
@@ -335,29 +365,28 @@
                 index = jnp.where(where == level + stage * facing[parity], number, index)
         wanted.append(index)
     sends = choose(jnp.stack(wanted), sources, chip_count)
-    rows = {
-        offset: across(sends[offset], offset) if offset else sends[offset]
-        for offset in range(chip_count)
-    }
-
-    parts = {}
-    for group in (several, bits, [0]):
-        made = project_parts(
-            core, [rows[offset] for offset in group], halves_of(group),
-            [cut] * (2 * len(group)), qkv_weight, other_weight,
-        )
-        for place, offset in enumerate(group):
-            parts[offset] = [part.astype(F32) for part in made[2 * place:2 * place + 2]]
-    for offset in reversed(several):
-        low, high = low_high(offset)
-        for part, (near, link) in enumerate(((offset ^ low, low), (offset ^ high, high))):
-            piece = across(parts[offset][part].astype(BF16), link)
-            parts[near][part] = parts[near][part] + piece.astype(F32)
-    for bit in bits:
-        for part in (0, 1):
-            piece = across(parts[bit][part].astype(BF16), bit)
-            parts[0][part] = parts[0][part] + piece.astype(F32)
-    projected = jnp.concatenate([part.astype(BF16) for part in parts[0]], axis=0)
+    rows = {offset: across(sends[offset], offset) if offset else sends[offset] for offset in range(chip_count)}
+
+    pieces = {(offset, part): [] for offset in range(chip_count) for part in (0, 1)}
+
+    def project(places):
+        items = [(rows[offset], part, grads[offset][part], pieces[offset, part] if offset else []) for offset, part in places]
+        made = project_parts(core, items, qkv_weight, other_weight)
+        return dict(zip(places, made))
+
+    own_parts = project([(0, 0), (0, 1)])
+    for weight in range(len(bits), 0, -1):
+        places = [(offset, part) for offset in offsets if bin(offset).count("1") == weight for part in (0, 1)]
+        bare = [place for place in places if not pieces[place]]
+        summed = [place for place in places if pieces[place]]
+        for some in (bare, summed):
+            made = project(some) if some else {}
+            for (offset, part), value in made.items():
+                link = low_high(offset)[part]
+                if offset in bits:
+                    link = offset
+                pieces[offset ^ link, part].append(across(value, link))
+    projected = finish([own_parts[0, 0], *pieces[0, 0]], [own_parts[0, 1], *pieces[0, 1]])
 
     near = [rows[offset] for offset in range(chip_count)]
     far = [sibling(block) for block in near]

time: 209 us -> 183 us (0.88)
  waiting for transfers between devices: 81 us -> 48.6 us
  local copies, waits for them, and re-layouts: 16.6 us -> 6.1 us
  Pallas kernels: 58.5 us -> 68.5 us
  starting transfers between devices: 43.5 us -> 47.1 us
  other arithmetic: 7.37 us -> 10.3 us
    ppermute x18, waiting for transfers between devices: 51.8 us -> 22.3 us  [across(): return lax.ppermute(value, 'loop', pairs)]
    unnamed x60 -> x54, local copies, waits for them, and re-layouts: 16.6 us -> 6.1 us
    pallas_call x3 -> x5, Pallas kernels: 20.4 us -> 28 us  [the longest x4 24.5 us: project_parts(): pl.pallas_call(functools.partial(project_kernel, counts=[len(item[3]) for...]
    ppermute x10, starting transfers between devices: 18.1 us -> 22.4 us  [along(): return lax.ppermute(value, 'tp', pairs)]
    convert_element_type x2, other arithmetic: 2.23 us -> 5.29 us  [body(): back[parity, stage] = along(value.astype(BF16), [(b, a) for a, b in pairs])]
    ppermute x10, waiting for transfers between devices: 28.4 us -> 26.3 us  [along(): return lax.ppermute(value, 'tp', pairs)]
  transfers between devices with their start and end apart: 41 -> 41, of which waited for: 14 -> 10; matrix products, arithmetic and copies ran while one was open for 3% -> 4% of each run, Pallas kernels for 28% -> 38%
where the time goes in v3:
time: 183 us; the launch traced here: 182 us
  Pallas kernels  68.5 us (37%)
  waiting for transfers between devices  48.6 us (27%)
  starting transfers between devices  47.1 us (26%)
  other arithmetic  10.3 us (6%)
  local copies, waits for them, and re-layouts  6.1 us (3%)
    ppermute x10, waiting for transfers between devices, along(): return lax.ppermute(value, 'tp', pairs)  26.3 us
    pallas_call x4, Pallas kernels, project_parts(): pl.pallas_call(functools.partial(project_kernel, counts=[len(item[3]) for...  24.5 us
    ppermute x10, starting transfers between devices, along(): return lax.ppermute(value, 'tp', pairs)  22.4 us
    ppermute x18, waiting for transfers between devices, across(): return lax.ppermute(value, 'loop', pairs)  22.3 us
    ppermute x18, starting transfers between devices, across(): return lax.ppermute(value, 'loop', pairs)  22.3 us
    pallas_call x3, Pallas kernels, input_terms(): pl.pallas_call(functools.partial(input_kernel, blocks=len(blocks), tile=t...  19.7 us
    pallas_call x1, Pallas kernels, weight_gradient(): pl.pallas_call(functools.partial(weight_kernel, blocks=len(blocks), grads...  15.8 us
    unnamed x54, local copies, waits for them, and re-layouts  6.1 us
  transfers between devices with their start and end apart: 41, of which 10 were waited for; matrix products, arithmetic and copies ran while one was open for 4% of the time, Pallas kernels for 38%

profile of v3, /device:TPU:0, one launch (start us, length us, event | category | flops | bytes accessed | tf_op | source)
XLA Modules:
  0.0 181.6 jit_solution(1333716850670112630)
XLA Ops:
  1.8 1.7 shard_map.77
  3.6 2.6 %collective-permute-start.12 = (bf16[136,1536]{1,0:T(8,128)(2,1)S(1)}, bf16[136,1536]{1,0:T(8,128)(2,1)S(1)}, u32[]{:S(2)}, u32[]{:S(2)}) collective-permute-start(bf16[136,1536]{1,0:T(8,128)(2,1)S(1)} %get-tuple-element.20.refs_2_.refs_0_.refs_8_.refs_24_), channel_id=1, source_target_pairs={{0,16},{4,20},{8,24},{12,28},{16,0},{20,4},{24,8},{28,12},{1,17},{... | collective-permute-start | bytes 1253384 | tf_op jit(solution)/shard_map/ppermute | solution.py:285
  6.2 1.5 collective-permute-start.8
  7.7 1.6 collective-permute-start.1
  9.8 6.7 %collective-permute-done.12.refs_3_.refs_2_.refs_12_.refs_28_ = bf16[136,1536]{1,0:T(8,128)(2,1)S(1)} collective-permute-done((bf16[136,1536]{1,0:T(8,128)(2,1)S(1)}, bf16[136,1536]{1,0:T(8,128)(2,1)S(1)}, u32[]{:S(2)}, u32[]{:S(2)}) %collective-permute-start.12) | collective-permute-done | bytes 417824 | tf_op jit(solution)/shard_map/ppermute | solution.py:285
  16.5 1.7 collective-permute-start.9
  23.1 3.8 %collective-permute-done.11.refs_2_.refs_1_.refs_11_.refs_27_ = bf16[136,1536]{1,0:T(8,128)(2,1)S(1)} collective-permute-done((bf16[136,1536]{1,0:T(8,128)(2,1)S(1)}, bf16[136,1536]{1,0:T(8,128)(2,1)S(1)}, u32[]{:S(2)}, u32[]{:S(2)}) %collective-permute-start.11) | collective-permute-done | bytes 417824 | tf_op jit(solution)/shard_map/ppermute | solution.py:285
  32.1 8.3 %shard_map.84 = (bf16[256,1024]{1,0:T(8,128)(2,1)S(1)}, bf16[256,1024]{1,0:T(8,128)(2,1)S(1)}) custom-call(s32[1]{0:T(128)} %bitcast.core, bf16[3,512,1536]{2,1,0:T(8,128)(2,1)} %own_weight.13, bf16[3,512,1536]{2,1,0:T(8,128)(2,1)} %collective-permute-done.other_weight, bf16[136,1536]{1,0:T(8,128)(2,1)} %copy-done.13, bf16[136,1536]{1,0:T(8,128)(2,1)} %copy-done.14, ...), custom_call_target="tpu_custom_call" | custom-call | tf_op jit(solution)/shard_map/pallas_call | solution.py:109
  42.5 5.6 %shard_map.83 = bf16[256,1024]{1,0:T(8,128)(2,1)S(1)} custom-call(s32[1]{0:T(128)} %bitcast.core, bf16[3,512,1536]{2,1,0:T(8,128)(2,1)} %own_weight.13, bf16[3,512,1536]{2,1,0:T(8,128)(2,1)} %collective-permute-done.other_weight, bf16[136,1536]{1,0:T(8,128)(2,1)} %collective-permute-done.14.refs_2_.refs_0_.refs_14_.refs_30_, ...), custom_call_target="tpu_custom_call" | custom-call | tf_op jit(solution)/shard_map/pallas_call | solution.py:109
  48.1 1.6 collective-permute-start.21
  49.6 11.2 %collective-permute-done.3.refs_3_ = bf16[256,1024]{1,0:T(8,128)(2,1)} collective-permute-done((bf16[256,1024]{1,0:T(8,128)(2,1)}, bf16[256,1024]{1,0:T(8,128)(2,1)}, u32[]{:S(2)}, u32[]{:S(2)}) %collective-permute-start.3) | collective-permute-done | bytes 524320 | tf_op jit(solution)/shard_map/ppermute | solution.py:300
  60.8 8.6 %collective-permute-done.5.refs_5_ = bf16[256,1024]{1,0:T(8,128)(2,1)} collective-permute-done((bf16[256,1024]{1,0:T(8,128)(2,1)}, bf16[256,1024]{1,0:T(8,128)(2,1)}, u32[]{:S(2)}, u32[]{:S(2)}) %collective-permute-start.5) | collective-permute-done | bytes 524320 | tf_op jit(solution)/shard_map/ppermute | solution.py:300
  70.8 3.3 %shard_map.76 = (bf16[256,1024]{1,0:T(8,128)(2,1)S(1)}, bf16[256,1024]{1,0:T(8,128)(2,1)}, bf16[256,1024]{1,0:T(8,128)(2,1)S(1)}, bf16[256,1024]{1,0:T(8,128)(2,1)S(1)}) custom-call(s32[4]{0:T(128)S(1)} %pad_add_fusion.wanted, bf16[256,1024]{1,0:T(8,128)(2,1)} %refs_0_.1, bf16[256,1024]{1,0:T(8,128)(2,1)} %copy-done.25, ...), custom_call_target="tpu_custom_call" | custom-call | tf_op jit(solution)/shard_map/pallas_call | solution.py:203
  74.1 5.8 %shard_map.85 = bf16[256,1024]{1,0:T(8,128)(2,1)S(1)} custom-call(s32[1]{0:T(128)} %bitcast.core, bf16[3,512,1536]{2,1,0:T(8,128)(2,1)} %own_weight.13, bf16[3,512,1536]{2,1,0:T(8,128)(2,1)} %collective-permute-done.other_weight, bf16[136,1536]{1,0:T(8,128)(2,1)} %copy-done, bf16[136,1536]{1,0:T(8,128)(2,1)} %copy-done.1), custom_call_target="tpu_custom_call" | custom-call | tf_op jit(solution)/shard_map/pallas_call | solution.py:109
  80.2 2.3 %select_select_fusion.1 = (bf16[256,1024]{1,0:T(8,128)(2,1)}, bf16[256,1024]{1,0:T(8,128)(2,1)}) fusion(bf16[256,1024]{1,0:T(8,128)(2,1)} %collective-permute-done.21, bf16[256,1024]{1,0:T(8,128)(2,1)S(1)} %copy-done.7, bf16[256,1024]{1,0:T(8,128)(2,1)S(1)} %copy-done.10, bf16[256,1024]{1,0:T(8,128)(2,1)S(1)} %shard_map.85, pred[]{:T(512)S(6)} %eq.156, ...), kind=kLoop, calls=%fused_computation.5 | loop fusion | flops 1572864 | bytes 3145734 | tf_op jit(solution)/shard_map/jit(_where)/select_n | solution.py:339
  83.9 7.1 %collective-permute-start.24 = (bf16[256,1024]{1,0:T(8,128)(2,1)}, bf16[256,1024]{1,0:T(8,128)(2,1)}, u32[]{:S(2)}, u32[]{:S(2)}) collective-permute-start(bf16[256,1024]{1,0:T(8,128)(2,1)} %get-tuple-element.37), channel_id=1, source_target_pairs={{0,1},{3,2},{4,5},{7,6},{8,9},{11,10},{12,13},{15,14},{16,17},{19,... | collective-permute-start | bytes 1572872 | tf_op jit(solution)/shard_map/ppermute | solution.py:300
  92.3 1.5 collective-permute-start.7
  94.5 2.5 %collective-permute-done.6.refs_0_.refs_1_ = bf16[256,1024]{1,0:T(8,128)(2,1)S(1)} collective-permute-done((bf16[256,1024]{1,0:T(8,128)(2,1)}, bf16[256,1024]{1,0:T(8,128)(2,1)S(1)}, u32[]{:S(2)}, u32[]{:S(2)}) %collective-permute-start.6) | collective-permute-done | bytes 524320 | tf_op jit(solution)/shard_map/ppermute | solution.py:285
  97.1 5.0 %collective-permute-done.24 = bf16[256,1024]{1,0:T(8,128)(2,1)} collective-permute-done((bf16[256,1024]{1,0:T(8,128)(2,1)}, bf16[256,1024]{1,0:T(8,128)(2,1)}, u32[]{:S(2)}, u32[]{:S(2)}) %collective-permute-start.24) | collective-permute-done | bytes 524320 | tf_op jit(solution)/shard_map/ppermute | solution.py:300
  102.1 4.4 %collective-permute-start.27 = (bf16[256,1024]{1,0:T(8,128)(2,1)}, bf16[256,1024]{1,0:T(8,128)(2,1)S(1)}, u32[]{:S(2)}, u32[]{:S(2)}) collective-permute-start(bf16[256,1024]{1,0:T(8,128)(2,1)} %get-tuple-element.38), channel_id=1, source_target_pairs={{0,1},{3,2},{4,5},{7,6},{8,9},{11,10},{12,13},{15,14},{16,17},{19,... | collective-permute-start | bytes 1572872 | tf_op jit(solution)/shard_map/ppermute | solution.py:300
  106.5 2.3 %add_convert_fusion.3 = bf16[256,1024]{1,0:T(8,128)(2,1)} fusion(bf16[256,1024]{1,0:T(8,128)(2,1)} %collective-permute-done.24, bf16[256,1024]{1,0:T(8,128)(2,1)} %collective-permute-done.21, bf16[256,1024]{1,0:T(8,128)(2,1)} %copy-done.6, bf16[256,1024]{1,0:T(8,128)(2,1)} %copy-done.9, bf16[256,1024]{1,0:T(8,128)(2,1)S(1)} %shard_map.85, pred[]{:T(512)S(6)} %eq.153, ...), kind=kLoop, calls=%fused_computation.3 | loop fusion | flops 1835008 | bytes 3145731 | tf_op jit(solution)/shard_map/convert_element_type | solution.py:350
  108.8 8.7 %collective-permute-done.7.refs_1_.refs_2_ = bf16[256,1024]{1,0:T(8,128)(2,1)} collective-permute-done((bf16[256,1024]{1,0:T(8,128)(2,1)S(1)}, bf16[256,1024]{1,0:T(8,128)(2,1)}, u32[]{:S(2)}, u32[]{:S(2)}) %collective-permute-start.7) | collective-permute-done | bytes 524320 | tf_op jit(solution)/shard_map/ppermute | solution.py:285
  120.4 5.9 %shard_map.80 = (bf16[128,1536]{1,0:T(8,128)(2,1)S(1)}, bf16[128,1536]{1,0:T(8,128)(2,1)S(1)}) custom-call(s32[1]{0:T(128)} %bitcast.core, bf16[3,512,1536]{2,1,0:T(8,128)(2,1)} %own_weight.13, bf16[3,512,1536]{2,1,0:T(8,128)(2,1)} %collective-permute-done.other_weight, bf16[256,1024]{1,0:T(8,128)(2,1)} %collective-permute-done.13.refs_0_.refs_1_.refs_3_, ...), custom_call_target="tpu_custom_call" | custom-call | tf_op jit(solution)/shard_map/pallas_call | solution.py:152
  126.4 1.6 collective-permute-start.16
  129.3 6.1 %shard_map.79 = (bf16[128,1536]{1,0:T(8,128)(2,1)S(1)}, bf16[128,1536]{1,0:T(8,128)(2,1)S(1)}) custom-call(s32[1]{0:T(128)} %bitcast.core, bf16[3,512,1536]{2,1,0:T(8,128)(2,1)} %own_weight.13, bf16[3,512,1536]{2,1,0:T(8,128)(2,1)} %collective-permute-done.other_weight, bf16[256,1024]{1,0:T(8,128)(2,1)} %copy-done.17, ...), custom_call_target="tpu_custom_call" | custom-call | tf_op jit(solution)/shard_map/pallas_call | solution.py:152
  135.4 1.5 collective-permute-start.10
  137.0 3.0 %add_convert_fusion.2 = (bf16[256,1024]{1,0:T(8,128)(2,1)}, bf16[256,1024]{1,0:T(8,128)(2,1)}) fusion(bf16[256,1024]{1,0:T(8,128)(2,1)} %collective-permute-done.25, bf16[256,1024]{1,0:T(8,128)(2,1)} %collective-permute-done.21, bf16[256,1024]{1,0:T(8,128)(2,1)S(1)} %copy-done.8, bf16[256,1024]{1,0:T(8,128)(2,1)S(1)} %copy-done.11, ...), kind=kLoop, calls=%fused_computation.2 | loop fusion | flops 3670016 | bytes 4194310 | tf_op jit(solution)/shard_map/convert_element_type | solution.py:350
  142.3 6.5 %shard_map.81 = (bf16[128,1536]{1,0:T(8,128)(2,1)S(1)}, bf16[128,1536]{1,0:T(8,128)(2,1)S(1)}) custom-call(s32[1]{0:T(128)} %bitcast.core, bf16[3,512,1536]{2,1,0:T(8,128)(2,1)} %own_weight.13, bf16[3,512,1536]{2,1,0:T(8,128)(2,1)} %collective-permute-done.other_weight, bf16[256,1024]{1,0:T(8,128)(2,1)} %copy-done.17, ...), custom_call_target="tpu_custom_call" | custom-call | tf_op jit(solution)/shard_map/pallas_call | solution.py:152
  152.2 15.8 %shard_map.86 = bf16[3,512,1536]{2,1,0:T(8,128)(2,1)} custom-call(s32[1]{0:T(128)} %bitcast.core, bf16[256,1024]{1,0:T(8,128)(2,1)} %copy-done.2, bf16[256,1024]{1,0:T(8,128)(2,1)} %copy-done.17, bf16[256,1024]{1,0:T(8,128)(2,1)} %collective-permute-done.7.refs_1_.refs_2_, bf16[256,1024]{1,0:T(8,128)(2,1)} %collective-permute-done.13.refs_0_.refs_1_.refs_3_, ...), custom_call_target="tpu_custom_call" | custom-call | tf_op jit(solution)/shard_map/pallas_call | solution.py:247
  168.0 6.0 %shard_map.78 = (bf16[128,1536]{1,0:T(8,128)(2,1)S(1)}, bf16[128,1536]{1,0:T(8,128)(2,1)S(1)}) custom-call(s32[1]{0:T(128)} %bitcast.core, bf16[3,512,1536]{2,1,0:T(8,128)(2,1)} %own_weight.13, bf16[3,512,1536]{2,1,0:T(8,128)(2,1)} %collective-permute-done.other_weight, bf16[256,1024]{1,0:T(8,128)(2,1)} %copy-done.2, bf16[256,1024]{1,0:T(8,128)(2,1)} %copy-done.2, ...), custom_call_target="tpu_custom_call" | custom-call | tf_op jit(solution)/shard_map/pallas_call | solution.py:152
  175.5 3.5 %shard_map.82 = bf16[256,1536]{1,0:T(8,128)(2,1)} custom-call(bf16[128,1536]{1,0:T(8,128)(2,1)} %copy-done.3, bf16[128,1536]{1,0:T(8,128)(2,1)} %copy-done.26, bf16[128,1536]{1,0:T(8,128)(2,1)} %collective-permute-done.18.refs_2_, bf16[128,1536]{1,0:T(8,128)(2,1)} %copy-done.4, bf16[128,1536]{1,0:T(8,128)(2,1)} %collective-permute-done.19.refs_4_, ...), custom_call_target="tpu_custom_call" | custom-call | tf_op jit(solution)/shard_map/pallas_call | solution.py:182
  179.0 2.6 %add_convert_fusion = bf16[256,1024]{1,0:T(8,128)(2,1)} fusion(bf16[256,1024]{1,0:T(8,128)(2,1)} %collective-permute-done.28, bf16[256,1024]{1,0:T(8,128)(2,1)} %collective-permute-done.26, bf16[256,1024]{1,0:T(8,128)(2,1)} %collective-permute-done.21, bf16[256,1024]{1,0:T(8,128)(2,1)S(1)} %copy-done.8, bf16[256,1024]{1,0:T(8,128)(2,1)S(1)} %copy-done.11, ...), kind=kLoop, calls=%fused_computation | loop fusion | flops 2359296 | bytes 3670019 | tf_op jit(solution)/shard_map/convert_element_type | solution.py:355
  (120 shorter events, 30.4 us)
Async XLA Ops:
  0.6 30.1 %collective-permute-start = (bf16[3,512,1536]{2,1,0:T(8,128)(2,1)}, bf16[3,512,1536]{2,1,0:T(8,128)(2,1)}, u32[]{:S(2)}, u32[]{:S(2)}) collective-permute-start(bf16[3,512,1536]{2,1,0:T(8,128)(2,1)} %own_weight.13), channel_id=1, source_target_pairs={{0,4},{4,0},{8,12},{12,8},{16,20},{20,16},{24,28},{28,24},{1,5},{5... | collective-permute-start | bytes 14155784 | tf_op jit(solution)/shard_map/ppermute | solution.py:288
  7.7 14.0 %collective-permute-start.1 = (bf16[256,1024]{1,0:T(8,128)(2,1)}, bf16[256,1024]{1,0:T(8,128)(2,1)S(1)}, u32[]{:S(2)}, u32[]{:S(2)}) collective-permute-start(bf16[256,1024]{1,0:T(8,128)(2,1)} %refs_0_.1), channel_id=1, source_target_pairs={{0,1},{1,0},{2,3},{3,2},{4,5},{5,4},{6,7},{7,6},{8,9},{9,8},{10,11... | collective-permute-start | bytes 1572872 | tf_op jit(solution)/shard_map/ppermute | solution.py:300
  9.3 17.6 %collective-permute-start.11 = (bf16[136,1536]{1,0:T(8,128)(2,1)S(1)}, bf16[136,1536]{1,0:T(8,128)(2,1)S(1)}, u32[]{:S(2)}, u32[]{:S(2)}) collective-permute-start(bf16[136,1536]{1,0:T(8,128)(2,1)S(1)} %get-tuple-element.21.refs_3_.refs_1_.refs_9_.refs_25_), channel_id=1, source_target_pairs={{0,8},{4,12},{8,0},{12,4},{16,24},{20,28},{24,16},{28,20},{1,9},{5... | collective-permute-start | bytes 1253384 | tf_op jit(solution)/shard_map/ppermute | solution.py:285
  26.9 13.5 %collective-permute-start.14 = (bf16[136,1536]{1,0:T(8,128)(2,1)S(1)}, bf16[136,1536]{1,0:T(8,128)(2,1)}, u32[]{:S(2)}, u32[]{:S(2)}) collective-permute-start(bf16[136,1536]{1,0:T(8,128)(2,1)S(1)} %collective-permute-done.12.refs_3_.refs_2_.refs_12_.refs_28_), channel_id=1, source_target_pairs={{0,8},{4,12},{8,0},{12,4},{16,24},{20,28},{24,16},{28,20},{1,9},{5... | collective-permute-start | bytes 1253384 | tf_op jit(solution)/shard_map/ppermute | solution.py:285
  28.4 13.1 %collective-permute-start.15 = (bf16[136,1536]{1,0:T(8,128)(2,1)S(1)}, bf16[136,1536]{1,0:T(8,128)(2,1)}, u32[]{:S(2)}, u32[]{:S(2)}) collective-permute-start(bf16[136,1536]{1,0:T(8,128)(2,1)S(1)} %collective-permute-done.11.refs_2_.refs_1_.refs_11_.refs_27_), channel_id=1, source_target_pairs={{0,16},{4,20},{8,24},{12,28},{16,0},{20,4},{24,8},{28,12},{1,17},{... | collective-permute-start | bytes 1253384 | tf_op jit(solution)/shard_map/ppermute | solution.py:285
  29.4 18.6 %collective-permute-start.33 = (bf16[136,1536]{1,0:T(8,128)(2,1)S(1)}, bf16[136,1536]{1,0:T(8,128)(2,1)}, u32[]{:S(2)}, u32[]{:S(2)}) collective-permute-start(bf16[136,1536]{1,0:T(8,128)(2,1)S(1)} %get-tuple-element.20.refs_2_.refs_0_.refs_8_.refs_24_), channel_id=1, source_target_pairs={{0,4},{4,0},{8,12},{12,8},{16,20},{20,16},{24,28},{28,24},{1,5},{5... | collective-permute-start | bytes 1253384 | tf_op jit(solution)/shard_map/ppermute | solution.py:288
  29.4 31.4 %collective-permute-start.3 = (bf16[256,1024]{1,0:T(8,128)(2,1)}, bf16[256,1024]{1,0:T(8,128)(2,1)}, u32[]{:S(2)}, u32[]{:S(2)}) collective-permute-start(bf16[256,1024]{1,0:T(8,128)(2,1)} %collective-permute-done.2.refs_2_), channel_id=1, source_target_pairs={{1,0},{2,3},{5,4},{6,7},{9,8},{10,11},{13,12},{14,15},{17,16},{18,... | collective-permute-start | bytes 1572872 | tf_op jit(solution)/shard_map/ppermute | solution.py:300
  30.7 38.6 %collective-permute-start.5 = (bf16[256,1024]{1,0:T(8,128)(2,1)}, bf16[256,1024]{1,0:T(8,128)(2,1)}, u32[]{:S(2)}, u32[]{:S(2)}) collective-permute-start(bf16[256,1024]{1,0:T(8,128)(2,1)} %collective-permute-done.4.refs_4_), channel_id=1, source_target_pairs={{1,0},{2,3},{5,4},{6,7},{9,8},{10,11},{13,12},{14,15},{17,16},{18,... | collective-permute-start | bytes 1572872 | tf_op jit(solution)/shard_map/ppermute | solution.py:300
  40.4 29.0 %collective-permute-start.22 = (bf16[256,1024]{1,0:T(8,128)(2,1)S(1)}, bf16[256,1024]{1,0:T(8,128)(2,1)S(1)}, u32[]{:S(2)}, u32[]{:S(2)}) collective-permute-start(bf16[256,1024]{1,0:T(8,128)(2,1)S(1)} %get-tuple-element.33), channel_id=1, source_target_pairs={{0,16},{4,20},{8,24},{12,28},{16,0},{20,4},{24,8},{28,12},{1,17},{... | collective-permute-start | bytes 1572872 | tf_op jit(solution)/shard_map/ppermute | solution.py:285
  41.5 28.4 %collective-permute-start.23 = (bf16[256,1024]{1,0:T(8,128)(2,1)S(1)}, bf16[256,1024]{1,0:T(8,128)(2,1)S(1)}, u32[]{:S(2)}, u32[]{:S(2)}) collective-permute-start(bf16[256,1024]{1,0:T(8,128)(2,1)S(1)} %get-tuple-element.34), channel_id=1, source_target_pairs={{0,8},{4,12},{8,0},{12,4},{16,24},{20,28},{24,16},{28,20},{1,9},{5... | collective-permute-start | bytes 1572872 | tf_op jit(solution)/shard_map/ppermute | solution.py:285
  48.1 31.9 %collective-permute-start.21 = (bf16[256,1024]{1,0:T(8,128)(2,1)S(1)}, bf16[256,1024]{1,0:T(8,128)(2,1)}, u32[]{:S(2)}, u32[]{:S(2)}) collective-permute-start(bf16[256,1024]{1,0:T(8,128)(2,1)S(1)} %shard_map.83), channel_id=1, source_target_pairs={{0,24},{4,28},{8,16},{12,20},{16,8},{20,12},{24,0},{28,4},{1,25},{... | collective-permute-start | bytes 1572872 | tf_op jit(solution)/shard_map/ppermute | solution.py:285
  60.8 21.7 %collective-permute-start.34 = (bf16[136,1536]{1,0:T(8,128)(2,1)S(1)}, bf16[136,1536]{1,0:T(8,128)(2,1)}, u32[]{:S(2)}, u32[]{:S(2)}) collective-permute-start(bf16[136,1536]{1,0:T(8,128)(2,1)S(1)} %get-tuple-element.21.refs_3_.refs_1_.refs_9_.refs_25_), channel_id=1, source_target_pairs={{0,4},{4,0},{8,12},{12,8},{16,20},{20,16},{24,28},{28,24},{1,5},{5... | collective-permute-start | bytes 1253384 | tf_op jit(solution)/shard_map/ppermute | solution.py:288
  69.4 14.6 %collective-permute-start.37 = (bf16[136,1536]{1,0:T(8,128)(2,1)}, bf16[136,1536]{1,0:T(8,128)(2,1)}, u32[]{:S(2)}, u32[]{:S(2)}) collective-permute-start(bf16[136,1536]{1,0:T(8,128)(2,1)} %copy-done.12), channel_id=1, source_target_pairs={{0,4},{4,0},{8,12},{12,8},{16,20},{20,16},{24,28},{28,24},{1,5},{5... | collective-permute-start | bytes 1253384 | tf_op jit(solution)/shard_map/ppermute | solution.py:288
  69.4 21.7 %collective-permute-start.35 = (bf16[136,1536]{1,0:T(8,128)(2,1)}, bf16[136,1536]{1,0:T(8,128)(2,1)}, u32[]{:S(2)}, u32[]{:S(2)}) collective-permute-start(bf16[136,1536]{1,0:T(8,128)(2,1)} %copy-done.13), channel_id=1, source_target_pairs={{0,4},{4,0},{8,12},{12,8},{16,20},{20,16},{24,28},{28,24},{1,5},{5... | collective-permute-start | bytes 1253384 | tf_op jit(solution)/shard_map/ppermute | solution.py:288
  69.9 21.2 %collective-permute-start.36 = (bf16[136,1536]{1,0:T(8,128)(2,1)}, bf16[136,1536]{1,0:T(8,128)(2,1)}, u32[]{:S(2)}, u32[]{:S(2)}) collective-permute-start(bf16[136,1536]{1,0:T(8,128)(2,1)} %copy-done.14), channel_id=1, source_target_pairs={{0,4},{4,0},{8,12},{12,8},{16,20},{20,16},{24,28},{28,24},{1,5},{5... | collective-permute-start | bytes 1253384 | tf_op jit(solution)/shard_map/ppermute | solution.py:288
  82.5 14.6 %collective-permute-start.6 = (bf16[256,1024]{1,0:T(8,128)(2,1)}, bf16[256,1024]{1,0:T(8,128)(2,1)S(1)}, u32[]{:S(2)}, u32[]{:S(2)}) collective-permute-start(bf16[256,1024]{1,0:T(8,128)(2,1)} %get-tuple-element.23), channel_id=1, source_target_pairs={{0,8},{4,12},{8,0},{12,4},{16,24},{20,28},{24,16},{28,20},{1,9},{5... | collective-permute-start | bytes 1572872 | tf_op jit(solution)/shard_map/ppermute | solution.py:285
  83.9 18.1 %collective-permute-start.24 = (bf16[256,1024]{1,0:T(8,128)(2,1)}, bf16[256,1024]{1,0:T(8,128)(2,1)}, u32[]{:S(2)}, u32[]{:S(2)}) collective-permute-start(bf16[256,1024]{1,0:T(8,128)(2,1)} %get-tuple-element.37), channel_id=1, source_target_pairs={{0,1},{3,2},{4,5},{7,6},{8,9},{11,10},{12,13},{15,14},{16,17},{19,... | collective-permute-start | bytes 1572872 | tf_op jit(solution)/shard_map/ppermute | solution.py:300
  92.3 25.2 %collective-permute-start.7 = (bf16[256,1024]{1,0:T(8,128)(2,1)S(1)}, bf16[256,1024]{1,0:T(8,128)(2,1)}, u32[]{:S(2)}, u32[]{:S(2)}) collective-permute-start(bf16[256,1024]{1,0:T(8,128)(2,1)S(1)} %get-tuple-element.24), channel_id=1, source_target_pairs={{0,16},{4,20},{8,24},{12,28},{16,0},{20,4},{24,8},{28,12},{1,17},{... | collective-permute-start | bytes 1572872 | tf_op jit(solution)/shard_map/ppermute | solution.py:285
  93.8 25.2 %collective-permute-start.13 = (bf16[256,1024]{1,0:T(8,128)(2,1)S(1)}, bf16[256,1024]{1,0:T(8,128)(2,1)}, u32[]{:S(2)}, u32[]{:S(2)}) collective-permute-start(bf16[256,1024]{1,0:T(8,128)(2,1)S(1)} %get-tuple-element.26), channel_id=1, source_target_pairs={{0,24},{4,28},{8,16},{12,20},{16,8},{20,12},{24,0},{28,4},{1,25},{... | collective-permute-start | bytes 1572872 | tf_op jit(solution)/shard_map/ppermute | solution.py:285
  94.5 24.5 %collective-permute-start.29 = (bf16[256,1024]{1,0:T(8,128)(2,1)S(1)}, bf16[256,1024]{1,0:T(8,128)(2,1)S(1)}, u32[]{:S(2)}, u32[]{:S(2)}) collective-permute-start(bf16[256,1024]{1,0:T(8,128)(2,1)S(1)} %get-tuple-element.19.refs_0_.refs_1_), channel_id=1, source_target_pairs={{0,4},{4,0},{8,12},{12,8},{16,20},{20,16},{24,28},{28,24},{1,5},{5... | collective-permute-start | bytes 1572872 | tf_op jit(solution)/shard_map/ppermute | solution.py:288
  97.1 29.3 %collective-permute-start.30 = (bf16[256,1024]{1,0:T(8,128)(2,1)S(1)}, bf16[256,1024]{1,0:T(8,128)(2,1)S(1)}, u32[]{:S(2)}, u32[]{:S(2)}) collective-permute-start(bf16[256,1024]{1,0:T(8,128)(2,1)S(1)} %collective-permute-done.6.refs_0_.refs_1_), channel_id=1, source_target_pairs={{0,4},{4,0},{8,12},{12,8},{16,20},{20,16},{24,28},{28,24},{1,5},{5... | collective-permute-start | bytes 1572872 | tf_op jit(solution)/shard_map/ppermute | solution.py:288
  102.1 25.8 %collective-permute-start.27 = (bf16[256,1024]{1,0:T(8,128)(2,1)}, bf16[256,1024]{1,0:T(8,128)(2,1)S(1)}, u32[]{:S(2)}, u32[]{:S(2)}) collective-permute-start(bf16[256,1024]{1,0:T(8,128)(2,1)} %get-tuple-element.38), channel_id=1, source_target_pairs={{0,1},{3,2},{4,5},{7,6},{8,9},{11,10},{12,13},{15,14},{16,17},{19,... | collective-permute-start | bytes 1572872 | tf_op jit(solution)/shard_map/ppermute | solution.py:300
  117.6 17.8 %collective-permute-start.25 = (bf16[256,1024]{1,0:T(8,128)(2,1)}, bf16[256,1024]{1,0:T(8,128)(2,1)}, u32[]{:S(2)}, u32[]{:S(2)}) collective-permute-start(bf16[256,1024]{1,0:T(8,128)(2,1)} %add_convert_fusion.3), channel_id=1, source_target_pairs={{2,1},{1,2},{6,5},{5,6},{10,9},{9,10},{14,13},{13,14},{18,17},{17,... | collective-permute-start | bytes 1572872 | tf_op jit(solution)/shard_map/ppermute | solution.py:300
  119.1 29.8 %collective-permute-start.31 = (bf16[256,1024]{1,0:T(8,128)(2,1)}, bf16[256,1024]{1,0:T(8,128)(2,1)S(1)}, u32[]{:S(2)}, u32[]{:S(2)}) collective-permute-start(bf16[256,1024]{1,0:T(8,128)(2,1)} %collective-permute-done.7.refs_1_.refs_2_), channel_id=1, source_target_pairs={{0,4},{4,0},{8,12},{12,8},{16,20},{20,16},{24,28},{28,24},{1,5},{5... | collective-permute-start | bytes 1572872 | tf_op jit(solution)/shard_map/ppermute | solution.py:288
  119.9 29.8 %collective-permute-start.32 = (bf16[256,1024]{1,0:T(8,128)(2,1)}, bf16[256,1024]{1,0:T(8,128)(2,1)}, u32[]{:S(2)}, u32[]{:S(2)}) collective-permute-start(bf16[256,1024]{1,0:T(8,128)(2,1)} %collective-permute-done.13.refs_0_.refs_1_.refs_3_), channel_id=1, source_target_pairs={{0,4},{4,0},{8,12},{12,8},{16,20},{20,16},{24,28},{28,24},{1,5},{5... | collective-permute-start | bytes 1572872 | tf_op jit(solution)/shard_map/ppermute | solution.py:288
  126.4 13.6 %collective-permute-start.16 = (bf16[128,1536]{1,0:T(8,128)(2,1)S(1)}, bf16[128,1536]{1,0:T(8,128)(2,1)}, u32[]{:S(2)}, u32[]{:S(2)}) collective-permute-start(bf16[128,1536]{1,0:T(8,128)(2,1)S(1)} %get-tuple-element.27), channel_id=1, source_target_pairs={{0,16},{4,20},{8,24},{12,28},{16,0},{20,4},{24,8},{28,12},{1,17},{... | collective-permute-start | bytes 1179656 | tf_op jit(solution)/shard_map/ppermute | solution.py:285
  135.4 15.6 %collective-permute-start.10 = (bf16[128,1536]{1,0:T(8,128)(2,1)S(1)}, bf16[128,1536]{1,0:T(8,128)(2,1)S(1)}, u32[]{:S(2)}, u32[]{:S(2)}) collective-permute-start(bf16[128,1536]{1,0:T(8,128)(2,1)S(1)} %get-tuple-element.25), channel_id=1, source_target_pairs={{0,8},{4,12},{8,0},{12,4},{16,24},{20,28},{24,16},{28,20},{1,9},{5... | collective-permute-start | bytes 1179656 | tf_op jit(solution)/shard_map/ppermute | solution.py:285
  139.9 39.1 %collective-permute-start.26 = (bf16[256,1024]{1,0:T(8,128)(2,1)}, bf16[256,1024]{1,0:T(8,128)(2,1)}, u32[]{:S(2)}, u32[]{:S(2)}) collective-permute-start(bf16[256,1024]{1,0:T(8,128)(2,1)} %get-tuple-element.35), channel_id=1, source_target_pairs={{1,0},{0,1},{3,2},{2,3},{5,4},{4,5},{7,6},{6,7},{9,8},{8,9},{11,10... | collective-permute-start | bytes 1572872 | tf_op jit(solution)/shard_map/ppermute | solution.py:300
  140.9 38.1 %collective-permute-start.28 = (bf16[256,1024]{1,0:T(8,128)(2,1)}, bf16[256,1024]{1,0:T(8,128)(2,1)}, u32[]{:S(2)}, u32[]{:S(2)}) collective-permute-start(bf16[256,1024]{1,0:T(8,128)(2,1)} %get-tuple-element.36), channel_id=1, source_target_pairs={{2,1},{1,2},{6,5},{5,6},{10,9},{9,10},{14,13},{13,14},{18,17},{17,... | collective-permute-start | bytes 1572872 | tf_op jit(solution)/shard_map/ppermute | solution.py:300
  148.9 26.6 %collective-permute-start.19 = (bf16[128,1536]{1,0:T(8,128)(2,1)S(1)}, bf16[128,1536]{1,0:T(8,128)(2,1)}, u32[]{:S(2)}, u32[]{:S(2)}) collective-permute-start(bf16[128,1536]{1,0:T(8,128)(2,1)S(1)} %get-tuple-element.31), channel_id=1, source_target_pairs={{0,16},{4,20},{8,24},{12,28},{16,0},{20,4},{24,8},{28,12},{1,17},{... | collective-permute-start | bytes 1179656 | tf_op jit(solution)/shard_map/ppermute | solution.py:285
  149.7 25.8 %collective-permute-start.18 = (bf16[128,1536]{1,0:T(8,128)(2,1)S(1)}, bf16[128,1536]{1,0:T(8,128)(2,1)}, u32[]{:S(2)}, u32[]{:S(2)}) collective-permute-start(bf16[128,1536]{1,0:T(8,128)(2,1)S(1)} %get-tuple-element.29), channel_id=1, source_target_pairs={{0,16},{4,20},{8,24},{12,28},{16,0},{20,4},{24,8},{28,12},{1,17},{... | collective-permute-start | bytes 1179656 | tf_op jit(solution)/shard_map/ppermute | solution.py:285
  151.7 23.8 %collective-permute-start.20 = (bf16[128,1536]{1,0:T(8,128)(2,1)S(1)}, bf16[128,1536]{1,0:T(8,128)(2,1)}, u32[]{:S(2)}, u32[]{:S(2)}) collective-permute-start(bf16[128,1536]{1,0:T(8,128)(2,1)S(1)} %get-tuple-element.32), channel_id=1, source_target_pairs={{0,8},{4,12},{8,0},{12,4},{16,24},{20,28},{24,16},{28,20},{1,9},{5... | collective-permute-start | bytes 1179656 | tf_op jit(solution)/shard_map/ppermute | solution.py:285
  (36 other events, 356.1 us)
